TPU v7x, 768 devices: a whole 4x8x12 slice. The times are simulated.
768 devices in a mesh: dp: 24 (over z, core), fsdp: 32 (over x, y).
Axes of the slice: x: 4, y: 8, z: 12, core: 2. Of those that a mesh axis runs over, the one named last changes fastest.
Arguments:
- inputs: bfloat16 [12288, 8192], P('dp', 'fsdp'), may hold values from -6 to 6
- cotangent: bfloat16 [2, 12288, 1024], P(None, 'dp', 'fsdp'), may hold values from -0.29882812 to 0.29882812
- feedback: float32 [2, 24, 8192, 1024], P(None, 'dp', 'fsdp'), may hold values from -6 to 6
- q_init: float32 [2, 1024, 128], replicated, may hold values from -0.1875 to 0.1875
- factor_ranks: int32 [2], replicated, may hold values from 8 to 128, as said below
Outputs:
- factor_p: float32 [2, 8192, 128], P(None, 'fsdp')
- factor_q: float32 [2, 1024, 128], replicated
- new_error: float32 [2, 24, 8192, 1024], P(None, 'dp', 'fsdp')
Inputs may be any that keep to these rules, and one draw needn't show every extreme that they name: `factor_ranks`: some projection has rank 128.
All inputs are finite; a program needn't handle non-finite values.
Results may differ from a plain program's by a relative error of at most 0.0003.
Values may be sent and summed in bfloat16 or wider, within the bound.
A program may use at most 32 MiB of HBM per device.

v0:
```python
import functools

import jax
import jax.numpy as jnp
from jax import lax
from jax.sharding import Mesh
from jax.sharding import PartitionSpec as P

DP = ("dp_0", "dp_1")


PRECISE = lax.Precision.HIGHEST


def sent_to_all(shard, axis):
    count = lax.axis_size(axis)
    return lax.all_to_all(
        jnp.broadcast_to(shard[None], (count, *shard.shape)), axis, 0, 0, tiled=True
    )


def laid_out(pieces, dim):
    lengths = list(pieces.shape[1:])
    lengths[dim] *= pieces.shape[0]
    return jnp.moveaxis(pieces, 0, dim).reshape(lengths)


def collect(shard, axis, dim):
    pieces = sent_to_all(shard, axis)
    return laid_out(pieces, dim)


def over_axes(shard, axes):
    return functools.reduce(lax.psum, axes, shard)


def total_of_pieces(shard, axis):
    return lax.all_gather(shard, axis).sum(0)


def cut_along(shard, dim, count):
    before, after = (shard.shape[:dim], shard.shape[dim + 1 :])
    return jnp.moveaxis(shard.reshape(*before, count, -1, *after), dim, 0)


def sum_at_owner(shard, axis, dim):
    count = lax.axis_size(axis)
    pieces = lax.all_to_all(cut_along(shard, dim, count), axis, 0, 0, tiled=True)
    return jnp.sum(pieces, axis=0)


def taken_together(shard, axis):
    return sent_to_all(shard, axis).sum(axis=0)


def triangle_solve(lower_factor, right_side):
    return jax.scipy.linalg.solve_triangular(lower_factor, right_side, lower=True)


def local(inputs, cotangent, feedback, q_init, factor_ranks):
    rank_width = q_init.shape[2]
    local_grad = jnp.einsum(
        "td,mtk->mdk", inputs, collect(cotangent, "fsdp", 2), preferred_element_type=jnp.float32
    )
    full_grad = feedback[:, 0] + local_grad
    rank_mask = (jnp.arange(rank_width)[None, :] < factor_ranks[:, None]).astype(jnp.float32)
    masked_q = q_init * rank_mask[:, None, :]
    left_local = jnp.einsum("mdk,mkr->mdr", full_grad, masked_q, precision=PRECISE)
    left_sum = over_axes(left_local, DP)
    gram_local = jnp.einsum("mdr,mds->mrs", left_sum, left_sum, precision=PRECISE)
    gram_matrix = total_of_pieces(gram_local, "fsdp") + jax.vmap(jnp.diag)(1.0 - rank_mask)
    chol_lower = jnp.linalg.cholesky(gram_matrix)
    solved = jax.vmap(triangle_solve)(chol_lower, jnp.swapaxes(left_sum, 1, 2))
    factor_p = jnp.swapaxes(solved, 1, 2)
    right_local = jnp.einsum("mdk,mdr->mkr", full_grad, factor_p, precision=PRECISE)
    right_rows = sum_at_owner(right_local, "fsdp", 1)
    right_rows = taken_together(right_rows, DP)
    factor_q = collect(right_rows, "fsdp", 1)
    low_rank = jnp.einsum("mdr,mkr->mdk", factor_p, factor_q, precision=PRECISE)
    new_error = (full_grad - low_rank)[:, None]
    return (factor_p, factor_q, new_error)


def solution(mesh):
    torus = Mesh(mesh.devices.reshape(12, 2, mesh.shape["fsdp"]), ("dp_0", "dp_1", "fsdp"))
    placed = (P(DP, "fsdp"), P(None, DP, "fsdp"), P(None, DP, "fsdp", None), P(), P())
    return jax.shard_map(
        local,
        mesh=torus,
        in_specs=placed,
        out_specs=(P(None, "fsdp", None), P(), P(None, DP, "fsdp", None)),
        check_vma=False,
    )
```

profile of v0, /device:TPU:1, one launch (start us, length us, event | category | flops | bytes accessed | tf_op | source)
XLA Modules:
  0.0 496.7 jit_solution(7459638890072307101)
XLA Ops:
  7.2 2.5 broadcast_in_dim.53
  9.7 10.5 %all-to-all-start = ((bf16[32,2,512,32]{2,3,1,0:T(8,128)(2,1)}), bf16[32,2,512,32]{2,3,1,0:T(8,128)(2,1)S(1)}, u32[]{:S(2)}, u32[]{:S(2)}) async-start(bf16[32,2,512,32]{2,3,1,0:T(8,128)(2,1)} %broadcast_in_dim.53), calls=%async_computation | async-start | bytes 4194304 | tf_op jit(solution)/shard_map/all_to_all | solution.py:17
  20.2 2.9 copy.29
  23.2 43.1 %all-to-all-done = bf16[32,2,512,32]{2,3,1,0:T(8,128)(2,1)S(1)} async-done(((bf16[32,2,512,32]{2,3,1,0:T(8,128)(2,1)}), bf16[32,2,512,32]{2,3,1,0:T(8,128)(2,1)S(1)}, u32[]{:S(2)}, u32[]{:S(2)}) %all-to-all-start) | async-done | bytes 2097184 | tf_op jit(solution)/shard_map/all_to_all | solution.py:17
  66.6 1.3 copy-done.1
  67.9 0.7 bitcast_add_fusion
  69.1 4.2 fusion
  73.4 112.5 %all-reduce.3.cloned.1.call-done = f32[2,256,128]{2,1,0:T(8,128)} async-done(((f32[2,256,128]{2,1,0:T(8,128)}), f32[2,256,128]{2,1,0:T(8,128)}) %all-reduce.3.cloned.1.call-update) | async-done | bytes 262160 | tf_op jit(solution)/shard_map/psum | solution.py:34
  186.1 49.4 %all-reduce.5.cloned.1.call-done = f32[2,256,128]{2,1,0:T(8,128)} async-done(((f32[2,256,128]{2,1,0:T(8,128)}), f32[2,256,128]{2,1,0:T(8,128)}) %all-reduce.5.cloned.1.call-update) | async-done | bytes 262160 | tf_op jit(solution)/shard_map/psum | solution.py:34
  235.5 2.3 fusion.8
  238.0 90.1 %all-gather.3.cloned.1.call-done = f32[64,128,128]{2,1,0:T(8,128)} async-done(((f32[2,128,128]{2,1,0:T(8,128)}), f32[64,128,128]{2,1,0:T(8,128)}) %all-gather.3.cloned.1.call-update) | async-done | bytes 4194320 | tf_op jit(solution)/shard_map/all_gather | solution.py:38
  328.1 2.4 reduce_sum.29
  330.7 23.5 %custom-call.8 = f32[2,128,128]{2,1,0:T(8,128)S(1)} custom-call(f32[2,128,128]{2,1,0:T(8,128)S(1)} %fusion.7), custom_call_target="Cholesky" | custom-call | tf_op jit(solution)/shard_map/jit(cholesky)/cholesky | solution.py:72
  354.4 19.7 %custom-call.9 = f32[2,1,128,128]{2,3,1,0:T(8,128)S(1)} custom-call(f32[2,1,128,128]{3,2,1,0:T(8,128)S(1)} %select_bitcast_fusion), custom_call_target="InvertDiagBlocksLowerTriangular" | custom-call | tf_op jit(solution)/shard_map/vmap(jit(_solve_triangular))/triangular_solve | solution.py:57
  374.6 1.9 fusion.9
  376.6 27.5 %all_to_all.20 = f32[32,2,32,128]{3,2,1,0:T(8,128)S(1)} all-to-all(f32[32,2,32,128]{3,2,1,0:T(8,128)S(1)} %bitcast.43), channel_id=1, replica_groups=mesh['dp_0'=12,'dp_1'=2,'fsdp'=32] {'fsdp'}, dimensions={0} | all-to-all | bytes 2097152 | tf_op jit(solution)/shard_map/all_to_all | solution.py:48
  404.2 48.8 %all_to_all.21 = f32[24,2,32,128]{3,2,1,0:T(8,128)S(1)} all-to-all(f32[24,2,32,128]{3,2,1,0:T(8,128)S(1)} %broadcast_in_dim.58), channel_id=1, replica_groups=mesh['dp_0'=12,'dp_1'=2,'fsdp'=32] {'dp_0','dp_1'}, dimensions={0} | all-to-all | bytes 1572864 | tf_op jit(solution)/shard_map/all_to_all | solution.py:17
  453.1 1.1 broadcast_in_dim.59
  454.2 4.8 all-to-all-start.3
  459.0 1.8 copy.39
  460.7 22.3 %all-to-all-done.3 = f32[32,2,32,128]{3,2,1,0:T(8,128)S(1)} async-done(((f32[32,2,32,128]{3,2,1,0:T(8,128)}), f32[32,2,32,128]{3,2,1,0:T(8,128)S(1)}, u32[]{:S(2)}, u32[]{:S(2)}) %all-to-all-start.3) | async-done | bytes 1048608 | tf_op jit(solution)/shard_map/all_to_all | solution.py:17
  483.1 1.0 copy-done.2
  484.1 3.2 subtract_bitcast_fusion
  487.3 2.9 copy.40
  (36 shorter events, 2.5 us)
Async XLA Ops:
  7.2 59.4 %copy-start = (bf16[512,256]{1,0:T(8,128)(2,1)S(1)}, bf16[512,256]{1,0:T(8,128)(2,1)}, u32[]{:S(2)}) copy-start(bf16[512,256]{1,0:T(8,128)(2,1)} %param.5) | copy-start | bytes 786436
  9.7 56.7 %all-to-all-start = ((bf16[32,2,512,32]{2,3,1,0:T(8,128)(2,1)}), bf16[32,2,512,32]{2,3,1,0:T(8,128)(2,1)S(1)}, u32[]{:S(2)}, u32[]{:S(2)}) async-start(bf16[32,2,512,32]{2,3,1,0:T(8,128)(2,1)} %broadcast_in_dim.53), calls=%async_computation | async-start | bytes 4194304 | tf_op jit(solution)/shard_map/all_to_all | solution.py:17
  20.2 2.9 copy-start.7
  20.2 165.7 %all-reduce.3.cloned.1.call-start = ((), (), s32[]{:S(2)}) async-start(), calls=%async_computation.4 | async-start | bytes 524288 | tf_op jit(solution)/shard_map/psum | solution.py:34
  66.3 1.6 copy-start.1
  67.9 1.2 copy-start.6
  73.3 162.2 %all-reduce.5.cloned.1.call-start = ((), (), s32[]{:S(2)}) async-start(), calls=%async_computation.5 | async-start | bytes 524288 | tf_op jit(solution)/shard_map/psum | solution.py:34
  185.9 142.2 %all-gather.3.cloned.1.call-start = ((), (), s32[]{:S(2)}) async-start(), calls=%async_computation.6 | async-start | bytes 4325376 | tf_op jit(solution)/shard_map/all_gather | solution.py:38
  328.1 46.0 %copy-start.5 = (f32[2,256,128]{2,1,0:T(8,128)S(1)}, f32[2,256,128]{2,1,0:T(8,128)}, u32[]{:S(2)}) copy-start(f32[2,256,128]{2,1,0:T(8,128)} %all-reduce.5.cloned.1.call-done) | copy-start | bytes 786436
  374.6 2.0 copy-start.3
  454.2 28.8 %all-to-all-start.3 = ((f32[32,2,32,128]{3,2,1,0:T(8,128)}), f32[32,2,32,128]{3,2,1,0:T(8,128)S(1)}, u32[]{:S(2)}, u32[]{:S(2)}) async-start(f32[32,2,32,128]{3,2,1,0:T(8,128)} %broadcast_in_dim.59), calls=%async_computation.3 | async-start | bytes 2097152 | tf_op jit(solution)/shard_map/all_to_all | solution.py:17
  483.0 1.1 copy-start.4
  483.1 1.0 copy-start.2
Sparse Core Ops, SparseCore 0:
  73.5 112.3 all-reduce.2
  189.0 46.4 all-reduce.4
  239.9 88.1 all-gather.2
where the time goes:
time: 501 us; the launch traced here: 497 us
  waiting for transfers between devices  317 us (63%)
  blocking collectives  76.3 us (15%)
  other arithmetic  46.2 us (9%)
  starting transfers between devices  15.6 us (3%)
  local copies, waits for them, and re-layouts  14.5 us (3%)
  between operations  13.9 us (3%)
  matrix products  12.7 us (3%)
    psum x2, waiting for transfers between devices, over_axes(): return functools.reduce(lax.psum, axes, shard)  162 us
    all_gather x1, waiting for transfers between devices, total_of_pieces(): return lax.all_gather(shard, axis).sum(0)  90.1 us
    all_to_all x2, waiting for transfers between devices, sent_to_all(): lax.all_to_all(jnp.broadcast_to(shard[None], (count, *shard.shape)), axis...  65.4 us
    all_to_all x1, blocking collectives, sent_to_all(): lax.all_to_all(jnp.broadcast_to(shard[None], (count, *shard.shape)), axis...  48.8 us
    all_to_all x1, blocking collectives, sum_at_owner(): lax.all_to_all(cut_along(shard, dim, count), axis, 0, 0, tiled=True)  27.5 us
    another operation x4, other arithmetic, local(): chol_lower = jnp.linalg.cholesky(gram_matrix)  23.6 us
    another operation x3, other arithmetic, triangle_solve(): jax.scipy.linalg.solve_triangular(lower_factor, right_side, lower=True)  19.8 us
    all_to_all x2, starting transfers between devices, sent_to_all(): lax.all_to_all(jnp.broadcast_to(shard[None], (count, *shard.shape)), axis...  15.3 us
  transfers between devices with their start and end apart: 5, of which 5 were waited for; matrix products, arithmetic and copies ran while one was open for 1% of the time, Pallas kernels for 0%

commit v1 on v0

v1 whole, which is shorter than its diff:
```python
import functools

import jax
import jax.numpy as jnp
from jax import lax
from jax.experimental import pallas as pl
from jax.experimental.pallas import tpu as pltpu
from jax.sharding import Mesh
from jax.sharding import PartitionSpec as P

MESH = pl.DeviceIdType.MESH
HI = lax.Precision.HIGHEST
NZ, NX, NY = 12, 4, 8
NF = NX * NY
PIECE = 24
DP = ("z", "c")
FS = ("x", "y")

OFFS = sorted(
    [(dx, dy) for dx in range(NX) for dy in range(NY) if dx or dy],
    key=lambda o: -(min(o[0], NX - o[0]) + min(o[1], NY - o[1])),
)
ZOFFS = sorted(range(1, NZ), key=lambda d: -min(d, NZ - d))


def nt(a, b, precision=HI):
    return lax.dot_general(
        a, b, (((1,), (1,)), ((), ())), precision=precision, preferred_element_type=jnp.float32
    )


def nn(a, b, precision=HI):
    return lax.dot_general(
        a, b, (((1,), (0,)), ((), ())), precision=precision, preferred_element_type=jnp.float32
    )


def comm_kernel(
    ranks, x_hbm, cot_hbm, fb_hbm, q_hbm,
    g_out, s_out, pf_out, li_out,
    xb, cv, cs, ct, fb, qv, gx, cf_t, pp, rs, pf3, s_src, s_rs, s_z, gl, g_rs, gg, mat,
    l_sem, pr_send, pr_recv, a_send, a_recv, b_send, b_recv, z_send, z_recv, f_send, f_recv,
):
    z, c, x, y = (lax.axis_index(n) for n in ("z", "c", "x", "y"))
    oc = 1 - c
    f = x * NY + y
    pending = []

    def at(dz=0, dx=0, dy=0):
        return (lax.rem(z + dz, NZ), c, lax.rem(x + dx, NX), lax.rem(y + dy, NY))

    partner = (z, oc, x, y)

    def send(src, dst, ssem, rsem, dev):
        cp = pltpu.make_async_remote_copy(
            src_ref=src, dst_ref=dst, send_sem=ssem, recv_sem=rsem, device_id=dev, device_id_type=MESH
        )
        cp.start()
        pending.append(cp)

    def arrive(dst, ssem, rsem, dev):
        pltpu.make_async_remote_copy(
            src_ref=dst, dst_ref=dst, send_sem=ssem, recv_sem=rsem, device_id=dev, device_id_type=MESH
        ).wait_recv()

    barrier = pltpu.get_barrier_semaphore()
    peers = [partner] + [at(dx=dx, dy=dy) for dx, dy in OFFS] + [at(dz=d) for d in ZOFFS]
    for peer in peers:
        pl.semaphore_signal(barrier, inc=1, device_id=peer, device_id_type=MESH)

    load_c = pltpu.make_async_copy(cot_hbm, cv, l_sem.at[0])
    load_x = pltpu.make_async_copy(x_hbm, xb.at[c], l_sem.at[1])
    load_f = pltpu.make_async_copy(fb_hbm.at[c, 0], fb.at[c], l_sem.at[2])
    load_q = pltpu.make_async_copy(q_hbm.at[c], qv, l_sem.at[3])
    load_c.start()
    load_x.start()
    load_f.start()
    load_q.start()

    load_c.wait()
    ct[c, x, y] = cv[c].astype(jnp.float32).T.astype(jnp.bfloat16)
    cs[...] = cv[oc].astype(jnp.float32).T.astype(jnp.bfloat16)

    pl.semaphore_wait(barrier, len(peers))

    send(cs, ct.at[c, x, y], pr_send.at[0], pr_recv.at[0], partner)

    def chunk(r, dx, dy):
        return ct.at[r, lax.rem(x + dx + NX, NX), lax.rem(y + dy + NY, NY)]

    def a_y(dirn, s):
        k = chunk(c, 0, -dirn * (s - 1))
        i = (s - 1) if dirn > 0 else 3 + s
        send(k, k, a_send.at[i], a_recv.at[i], at(dy=dirn % NY))

    def a_y_wait(dirn, s):
        i = (s - 1) if dirn > 0 else 3 + s
        arrive(chunk(c, 0, -dirn * s), a_send.at[i], a_recv.at[i], at(dy=-dirn % NY))

    def a_x(j, dirn):
        k = chunk(c, 0, -j)
        i = 8 + j * 3 + (0 if dirn > 0 else 1)
        send(k, k, a_send.at[i], a_recv.at[i], at(dx=dirn % NX))

    def a_x_wait(j, dirn):
        i = 8 + j * 3 + (0 if dirn > 0 else 1)
        arrive(chunk(c, -dirn, -j), a_send.at[i], a_recv.at[i], at(dx=-dirn % NX))

    def far_dir(j):
        return 1 if j % 2 == 0 else -1

    def a_x_far(j):
        d = far_dir(j)
        k = chunk(c, -d, -j)
        i = 8 + j * 3 + 2
        send(k, k, a_send.at[i], a_recv.at[i], at(dx=d % NX))

    def a_x_far_wait(j):
        d = far_dir(j)
        i = 8 + j * 3 + 2
        arrive(chunk(c, -2 * d, -j), a_send.at[i], a_recv.at[i], at(dx=-d % NX))

    def b_x(dx):
        k = chunk(oc, 0, 0)
        send(k, k, b_send.at[dx - 1], b_recv.at[dx - 1], at(dx=dx))

    def b_x_wait(dx):
        arrive(chunk(oc, -dx, 0), b_send.at[dx - 1], b_recv.at[dx - 1], at(dx=NX - dx))

    def b_reach(dx, dirn):
        return (4 if dirn > 0 else 3) if dx % 2 == 0 else (3 if dirn > 0 else 4)

    def b_idx(dx, dirn, s):
        return 3 + dx * 8 + (s - 1 if dirn > 0 else 3 + s)

    def b_y(dx, dirn, s):
        k = chunk(oc, -dx, -dirn * (s - 1))
        i = b_idx(dx, dirn, s)
        send(k, k, b_send.at[i], b_recv.at[i], at(dy=dirn % NY))

    def b_y_wait(dx, dirn, s):
        i = b_idx(dx, dirn, s)
        arrive(chunk(oc, -dx, -dirn * s), b_send.at[i], b_recv.at[i], at(dy=-dirn % NY))

    a_y(1, 1)
    a_y(-1, 1)
    a_x(0, 1)
    a_x(0, -1)

    arrive(ct.at[oc, x, y], pr_send.at[0], pr_recv.at[0], partner)
    for dx in (1, 3, 2):
        b_x(dx)
    b_y(0, 1, 1)
    b_y(0, -1, 1)
    load_x.wait()
    send(xb.at[c], xb.at[c], pr_send.at[1], pr_recv.at[1], partner)
    send(fb_hbm.at[oc, 0], fb.at[c], pr_send.at[2], pr_recv.at[2], partner)

    def y_of(j):
        return j

    a_x_done = []
    for s in range(1, 5):
        a_y_wait(1, s)
        if s < 4:
            a_y(1, s + 1)
        a_x(s, 1)
        a_x(s, -1)
        if s < 4:
            a_y_wait(-1, s)
            if s < 3:
                a_y(-1, s + 1)
            a_x(NY - s, 1)
            a_x(NY - s, -1)
        if s == 1:
            for dx in (1, 3, 2):
                b_x_wait(dx)
                b_y(dx, 1, 1)
                b_y(dx, -1, 1)
        for dx in (0, 1, 3, 2):
            for dirn in (1, -1):
                if s <= b_reach(dx, dirn):
                    b_y_wait(dx, dirn, s)
                    if s < b_reach(dx, dirn):
                        b_y(dx, dirn, s + 1)
        ready = {1: (0,), 2: (1, 7), 3: (2, 6), 4: (3, 5)}[s]
        for j in ready:
            d = far_dir(j)
            a_x_wait(j, d)
            a_x_far(j)
            a_x_wait(j, -d)
            a_x_done.append(j)
    d = far_dir(4)
    a_x_wait(4, d)
    a_x_far(4)
    a_x_wait(4, -d)
    for j in (0, 1, 7, 2, 6, 3, 5, 4):
        a_x_far_wait(j)

    load_f.wait()
    arrive(xb.at[oc], pr_send.at[1], pr_recv.at[1], partner)
    arrive(fb.at[oc], pr_send.at[2], pr_recv.at[2], partner)
    x_own = xb[c].astype(jnp.float32).T.astype(jnp.bfloat16)
    x_oth = xb[oc].astype(jnp.float32).T.astype(jnp.bfloat16)
    load_q.wait()
    width = lax.broadcasted_iota(jnp.int32, (1, 128), 1)
    rank = ranks[c]
    live = width < rank
    total = jnp.zeros((256, 128), jnp.float32)
    for b in range(NX):
        cols = pl.ds(b * 256, 256)
        own = fb[c, :, cols] + nt(x_own, ct[c, b].reshape(256, 512), None)
        oth = fb[oc, :, cols] + nt(x_oth, ct[oc, b].reshape(256, 512), None)
        g_out[c, :, cols] = own
        gx[:, cols] = oth
        both = own + oth
        total = total + nn(both, jnp.where(live, qv[cols, :], 0.0))
        cf_t[cols, :] = both.T
    for i in range(NZ):
        lo, hi = i * PIECE, min((i + 1) * PIECE, 256)
        if hi - lo == PIECE:
            pp[i] = total[lo:hi]
        elif hi > lo:
            pp[i, : hi - lo] = total[lo:hi]
            pp[i, hi - lo :] = jnp.zeros((PIECE - (hi - lo), 128), jnp.float32)
        else:
            pp[i] = jnp.zeros((PIECE, 128), jnp.float32)

    for d in ZOFFS:
        send(pp.at[lax.rem(z + d, NZ)], rs.at[d], z_send.at[d], z_recv.at[d], at(dz=d))
    send(gx, g_out.at[c], pr_send.at[3], pr_recv.at[3], partner)
    acc = pp[z]
    for d in reversed(ZOFFS):
        arrive(rs.at[d], z_send.at[d], z_recv.at[d], at(dz=NZ - d))
        acc = acc + rs[d]
    pf3[z] = acc
    for d in ZOFFS:
        send(pf3.at[z], pf3.at[z], z_send.at[12 + d], z_recv.at[12 + d], at(dz=d))
    for d in reversed(ZOFFS):
        zs = lax.rem(z + NZ - d, NZ)
        arrive(pf3.at[zs], z_send.at[12 + d], z_recv.at[12 + d], at(dz=NZ - d))
    left = pf3[...].reshape(NZ * PIECE, 128)[:256]
    pf_out[c] = left
    send(pf_out.at[c], pf_out.at[c], pr_send.at[4], pr_recv.at[4], partner)

    gram = nn(left.T, left)
    for i in range(NF):
        gl[i] = gram[4 * i : 4 * i + 4]
    for n, (dx, dy) in enumerate(OFFS):
        to = lax.rem(x + dx, NX) * NY + lax.rem(y + dy, NY)
        send(gl.at[to], g_rs.at[n], f_send.at[n], f_recv.at[n], at(dx=dx, dy=dy))
    for b in range(NX):
        rows = pl.ds(b * 256, 256)
        s_src[pl.ds(b * NY, NY)] = nn(cf_t[rows, :], left).reshape(NY, 32, 128)
    for n, (dx, dy) in enumerate(OFFS):
        to = lax.rem(x + dx, NX) * NY + lax.rem(y + dy, NY)
        send(s_src.at[to], s_rs.at[n], f_send.at[32 + n], f_recv.at[32 + n], at(dx=dx, dy=dy))

    def src(dx, dy):
        return at(dx=(NX - dx) % NX, dy=(NY - dy) % NY)

    acc = gl[f]
    for n, (dx, dy) in reversed(list(enumerate(OFFS))):
        arrive(g_rs.at[n], f_send.at[n], f_recv.at[n], src(dx, dy))
        acc = acc + g_rs[n]
    gg[f] = acc
    for n, (dx, dy) in enumerate(OFFS):
        send(gg.at[f], gg.at[f], f_send.at[64 + n], f_recv.at[64 + n], at(dx=dx, dy=dy))

    acc = s_src[f]
    for n, (dx, dy) in reversed(list(enumerate(OFFS))):
        arrive(s_rs.at[n], f_send.at[32 + n], f_recv.at[32 + n], src(dx, dy))
        acc = acc + s_rs[n]
    s_z[z] = acc
    for d in ZOFFS:
        send(s_z.at[z], s_z.at[z], z_send.at[24 + d], z_recv.at[24 + d], at(dz=d))

    for n, (dx, dy) in reversed(list(enumerate(OFFS))):
        sx, sy = lax.rem(x + NX - dx, NX), lax.rem(y + NY - dy, NY)
        arrive(gg.at[sx * NY + sy], f_send.at[64 + n], f_recv.at[64 + n], src(dx, dy))
    for i in range(NF):
        mat[4 * i : 4 * i + 4, :] = gg[i]
    row_id = lax.broadcasted_iota(jnp.int32, (128, 128), 0)
    col_id = lax.broadcasted_iota(jnp.int32, (128, 128), 1)
    mat[...] = mat[...] + jnp.where((row_id == col_id) & (col_id >= rank), 1.0, 0.0)

    def eliminate(j, carry):
        m = mat[...]
        row = mat[pl.ds(j, 1), :]
        hit = col_id == j
        hit1 = width == j
        pivot = jnp.sum(jnp.where(hit1, row, 0.0), axis=1, keepdims=True)
        col = jnp.sum(jnp.where(hit, m, 0.0), axis=1, keepdims=True)
        factor = jnp.where(row_id > j, col / pivot, 0.0)
        mat[...] = jnp.where(hit & (row_id > j), 0.0, m) - factor * jnp.where(hit1, 1.0, row)
        return carry

    lax.fori_loop(0, 64, eliminate, 0)

    for d in reversed(ZOFFS):
        zs = lax.rem(z + NZ - d, NZ)
        arrive(s_z.at[zs], z_send.at[24 + d], z_recv.at[24 + d], at(dz=NZ - d))
    acc = s_z[0]
    for i in range(1, NZ):
        acc = acc + s_z[i]
    s_out[c, f] = acc
    for n, (dx, dy) in enumerate(OFFS):
        send(s_out.at[c, f], s_out.at[c, f], f_send.at[96 + n], f_recv.at[96 + n], at(dx=dx, dy=dy))

    lax.fori_loop(64, 128, eliminate, 0)
    m = mat[...]
    diag = jnp.sum(jnp.where(row_id == col_id, m, 0.0), axis=1, keepdims=True)
    unit = jnp.where(row_id == col_id, 1.0, jnp.where(row_id > col_id, m, 0.0))
    li_out[c] = unit * (1.0 / jnp.sqrt(diag))
    send(li_out.at[c], li_out.at[c], pr_send.at[5], pr_recv.at[5], partner)

    for n, (dx, dy) in reversed(list(enumerate(OFFS))):
        sx, sy = lax.rem(x + NX - dx, NX), lax.rem(y + NY - dy, NY)
        arrive(s_out.at[c, sx * NY + sy], f_send.at[96 + n], f_recv.at[96 + n], src(dx, dy))
    send(s_out.at[c], s_out.at[c], pr_send.at[6], pr_recv.at[6], partner)
    arrive(g_out.at[oc], pr_send.at[3], pr_recv.at[3], partner)
    arrive(pf_out.at[oc], pr_send.at[4], pr_recv.at[4], partner)
    arrive(li_out.at[oc], pr_send.at[5], pr_recv.at[5], partner)
    arrive(s_out.at[oc], pr_send.at[6], pr_recv.at[6], partner)
    for cp in pending:
        cp.wait_send()


def final_kernel(g, s, pf, li, p_out, q_out, e_out):
    inv = li[0]
    left = nt(pf[0], inv)
    p_out[0] = left
    for b in range(4):
        rows = pl.ds(b * 256, 256)
        right = nt(s[0, rows, :], inv)
        q_out[0, rows, :] = right
        e_out[0, 0, :, rows] = g[0, :, rows] - nt(left, right)


def local(inputs, cotangent, feedback, q_init, factor_ranks):
    f32, b16 = jnp.float32, jnp.bfloat16
    vm = pl.BlockSpec(memory_space=pltpu.VMEM)
    anyspace = pl.BlockSpec(memory_space=pl.ANY)
    dma = pltpu.SemaphoreType.DMA
    g, s, pf, li = pl.pallas_call(
        comm_kernel,
        out_shape=(
            jax.ShapeDtypeStruct((2, 256, 1024), f32),
            jax.ShapeDtypeStruct((2, NF, 32, 128), f32),
            jax.ShapeDtypeStruct((2, 256, 128), f32),
            jax.ShapeDtypeStruct((2, 128, 128), f32),
        ),
        in_specs=[pl.BlockSpec(memory_space=pltpu.SMEM)] + [anyspace] * 4,
        out_specs=(vm,) * 4,
        scratch_shapes=[
            pltpu.VMEM((2, 512, 256), b16),
            pltpu.VMEM((2, 512, 32), b16),
            pltpu.VMEM((32, 512), b16),
            pltpu.VMEM((2, NX, NY, 32, 512), b16),
            pltpu.VMEM((2, 256, 1024), f32),
            pltpu.VMEM((1024, 128), f32),
            pltpu.VMEM((256, 1024), f32),
            pltpu.VMEM((1024, 256), f32),
            pltpu.VMEM((NZ, PIECE, 128), f32),
            pltpu.VMEM((NZ, PIECE, 128), f32),
            pltpu.VMEM((NZ, PIECE, 128), f32),
            pltpu.VMEM((NF, 32, 128), f32),
            pltpu.VMEM((NF, 32, 128), f32),
            pltpu.VMEM((NZ, 32, 128), f32),
            pltpu.VMEM((NF, 4, 128), f32),
            pltpu.VMEM((NF, 4, 128), f32),
            pltpu.VMEM((NF, 4, 128), f32),
            pltpu.VMEM((128, 128), f32),
            dma((4,)),
            dma((7,)), dma((7,)),
            dma((32,)), dma((32,)),
            dma((35,)), dma((35,)),
            dma((36,)), dma((36,)),
            dma((128,)), dma((128,)),
        ],
        compiler_params=pltpu.CompilerParams(
            collective_id=0, has_side_effects=True, vmem_limit_bytes=56 << 20
        ),
        name="exchange",
    )(factor_ranks, inputs, cotangent, feedback, q_init)
    s = s.reshape(2, 1024, 128)

    def whole(*shape):
        return pl.BlockSpec((1, *shape), lambda m: (m,) + (0,) * len(shape))

    return pl.pallas_call(
        final_kernel,
        grid=(2,),
        out_shape=(
            jax.ShapeDtypeStruct((2, 256, 128), f32),
            jax.ShapeDtypeStruct((2, 1024, 128), f32),
            jax.ShapeDtypeStruct((2, 1, 256, 1024), f32),
        ),
        in_specs=[whole(256, 1024), whole(1024, 128), whole(256, 128), whole(128, 128)],
        out_specs=(whole(256, 128), whole(1024, 128), whole(1, 256, 1024)),
        compiler_params=pltpu.CompilerParams(dimension_semantics=("arbitrary",)),
        name="finish",
    )(g, s, pf, li)


def solution(mesh):
    torus = Mesh(mesh.devices.reshape(NZ, 2, NX, NY), ("z", "c", "x", "y"))
    placed = (P(DP, FS), P(None, DP, FS), P(None, DP, FS, None), P(), P())
    return jax.shard_map(
        local,
        mesh=torus,
        in_specs=placed,
        out_specs=(P(None, FS, None), P(), P(None, DP, FS, None)),
        check_vma=False,
    )
```

time: 501 us -> 110 us (0.22)
  waiting for transfers between devices: 317 us -> 0 us
  Pallas kernels: 0 us -> 107 us
  blocking collectives: 76.3 us -> 0 us
  other arithmetic: 46.2 us -> 0 us
  starting transfers between devices: 15.6 us -> 0 us
  between operations: 13.9 us -> 0.64 us
  local copies, waits for them, and re-layouts: 14.5 us -> 1.68 us
  matrix products: 12.7 us -> 0 us
    psum x2 -> x0, waiting for transfers between devices: 162 us -> none  [over_axes(): return functools.reduce(lax.psum, axes, shard)]
    pallas_call x0 -> x2, Pallas kernels: none -> 107 us  [the longest x1 101 us: local(): pl.pallas_call(comm_kernel, out_shape=(jax.ShapeDtypeStruct((2, 256, 1024...]
    all_gather x1 -> x0, waiting for transfers between devices: 90.1 us -> none  [total_of_pieces(): return lax.all_gather(shard, axis).sum(0)]
    all_to_all x2 -> x0, blocking collectives: 76.3 us -> none  [the longest x1 48.8 us: sent_to_all(): lax.all_to_all(jnp.broadcast_to(shard[None], (count, *shard.shape)), axis...]
    all_to_all x2 -> x0, waiting for transfers between devices: 65.4 us -> none  [sent_to_all(): lax.all_to_all(jnp.broadcast_to(shard[None], (count, *shard.shape)), axis...]
    another operation x7 -> x0, other arithmetic: 43.4 us -> none  [the longest x4 23.6 us: local(): chol_lower = jnp.linalg.cholesky(gram_matrix)]
    all_to_all x2 -> x0, starting transfers between devices: 15.3 us -> none  [sent_to_all(): lax.all_to_all(jnp.broadcast_to(shard[None], (count, *shard.shape)), axis...]
    dot_general x5 -> x0, matrix products: 12.3 us -> none  [the longest x1 4.19 us: local(): jnp.einsum('mdk,mkr->mdr', full_grad, masked_q, precision=PRECISE)]
  transfers between devices with their start and end apart: 5 -> 0, of which waited for: 5 -> 0; matrix products, arithmetic and copies ran while one was open for 1% -> 0% of each run, Pallas kernels for 0% -> 0%
where the time goes in v1:
time: 110 us
  Pallas kernels  107 us (97%)
  local copies, waits for them, and re-layouts  1.68 us (2%)
    pallas_call x1, Pallas kernels, local(): pl.pallas_call(comm_kernel, out_shape=(jax.ShapeDtypeStruct((2, 256, 1024...  101 us
    pallas_call x1, Pallas kernels, local(): pl.pallas_call(final_kernel, grid=(2,), out_shape=(jax.ShapeDtypeStruct((...  6.03 us

profile of v1, /device:TPU:1, one launch (start us, length us, event | category | flops | bytes accessed | tf_op | source)
XLA Modules:
  0.0 109.7 jit_solution(10084568261628445640)
XLA Ops:
  0.6 1.7 %copy.8.cot_hbm = bf16[2,512,32]{2,1,0:T(8,128)(2,1)} copy(bf16[2,512,32]{1,2,0:T(8,128)(2,1)} %param.6) | data formatting | bytes 131072 | tf_op args[1]
  2.3 101.3 %exchange.1 = (f32[2,256,1024]{2,1,0:T(8,128)}, f32[2,32,32,128]{3,2,1,0:T(8,128)}, f32[2,256,128]{2,1,0:T(8,128)}, f32[2,128,128]{2,1,0:T(8,128)}) custom-call(s32[2]{0:T(128)} %ranks.1, bf16[512,256]{1,0:T(8,128)(2,1)} %x_hbm.1, bf16[2,512,32]{2,1,0:T(8,128)(2,1)} %copy.8.cot_hbm, f32[2,1,256,1024]{3,2,1,0:T(8,128)} %fb_hbm.1, f32[2,1024,128]{2,1,0:T(8,128)} %q_hbm.1), custom_call_target="tpu_custom_call" | custom-call | tf_op jit(solution)/shard_map/exchange/pallas_call | solution.py:345
  103.6 6.0 %finish.1 = (f32[2,256,128]{2,1,0:T(8,128)}, f32[2,1024,128]{2,1,0:T(8,128)}, f32[2,1,256,1024]{3,2,1,0:T(8,128)}) custom-call(f32[2,256,1024]{2,1,0:T(8,128)} %get-tuple-element.7.g, f32[2,1024,128]{2,1,0:T(8,128)} %bitcast.1, f32[2,256,128]{2,1,0:T(8,128)} %get-tuple-element.9.pf, f32[2,128,128]{2,1,0:T(8,128)} %get-tuple-element.10.li), custom_call_target="tpu_custom_call" | custom-call | tf_op jit(solution)/shard_map/finish/pallas_call | solution.py:391

commit v2 on v1

--- a/solution.py
+++ b/solution.py
@@ -35,11 +35,21 @@
     )
 
 
+def split(a):
+    high = a.astype(jnp.bfloat16)
+    return high, (a - high.astype(jnp.float32)).astype(jnp.bfloat16)
+
+
+def three(dot, a, b):
+    (ah, al), (bh, bl) = a, b
+    return dot(ah, bh, None) + (dot(ah, bl, None) + dot(al, bh, None))
+
+
 def comm_kernel(
     ranks, x_hbm, cot_hbm, fb_hbm, q_hbm,
     g_out, s_out, pf_out, li_out,
-    xb, cv, cs, ct, fb, qv, gx, cf_t, pp, rs, pf3, s_src, s_rs, s_z, gl, g_rs, gg, mat,
-    l_sem, pr_send, pr_recv, a_send, a_recv, b_send, b_recv, z_send, z_recv, f_send, f_recv,
+    xb, ct, fb, qv, gw, gx, cf_h, cf_l, pp, rs, pf3, s_src, s_rs, s_z, gl, g_rs, gg, mat,
+    l_sem, pr_send, pr_recv, a_send, a_recv, b_send, b_recv, z_send, z_recv, f_send, f_recv, near,
 ):
     z, c, x, y = (lax.axis_index(n) for n in ("z", "c", "x", "y"))
     oc = 1 - c
@@ -64,11 +74,12 @@
         ).wait_recv()
 
     barrier = pltpu.get_barrier_semaphore()
-    peers = [partner] + [at(dx=dx, dy=dy) for dx, dy in OFFS] + [at(dz=d) for d in ZOFFS]
+    peers = [partner] + [(z, oc, lax.rem(x + dx, NX), y) for dx in (1, 2, 3)]
+    peers += [at(dx=1), at(dx=NX - 1), at(dy=1), at(dy=NY - 1), at(dz=1), at(dz=NZ - 1)]
     for peer in peers:
         pl.semaphore_signal(barrier, inc=1, device_id=peer, device_id_type=MESH)
 
-    load_c = pltpu.make_async_copy(cot_hbm, cv, l_sem.at[0])
+    load_c = pltpu.make_async_copy(cot_hbm.at[c], ct.at[c, x, y], l_sem.at[0])
     load_x = pltpu.make_async_copy(x_hbm, xb.at[c], l_sem.at[1])
     load_f = pltpu.make_async_copy(fb_hbm.at[c, 0], fb.at[c], l_sem.at[2])
     load_q = pltpu.make_async_copy(q_hbm.at[c], qv, l_sem.at[3])
@@ -76,14 +87,18 @@
     load_x.start()
     load_f.start()
     load_q.start()
-
     load_c.wait()
-    ct[c, x, y] = cv[c].astype(jnp.float32).T.astype(jnp.bfloat16)
-    cs[...] = cv[oc].astype(jnp.float32).T.astype(jnp.bfloat16)
+    load_x.wait()
 
     pl.semaphore_wait(barrier, len(peers))
 
-    send(cs, ct.at[c, x, y], pr_send.at[0], pr_recv.at[0], partner)
+    def tell(r):
+        for n, dz in enumerate((1, NZ - 1)):
+            pl.semaphore_signal(near.at[r - 1, n], inc=1, device_id=at(dz=dz), device_id_type=MESH)
+
+    def told(r):
+        for n in range(2):
+            pl.semaphore_wait(near.at[r - 1, n], 1)
 
     def chunk(r, dx, dy):
         return ct.at[r, lax.rem(x + dx + NX, NX), lax.rem(y + dy + NY, NY)]
@@ -121,17 +136,16 @@
         arrive(chunk(c, -2 * d, -j), a_send.at[i], a_recv.at[i], at(dx=-d % NX))
 
     def b_x(dx):
-        k = chunk(oc, 0, 0)
-        send(k, k, b_send.at[dx - 1], b_recv.at[dx - 1], at(dx=dx))
+        send(cot_hbm.at[oc], ct.at[c, x, y], b_send.at[dx], b_recv.at[dx], (z, oc, lax.rem(x + dx, NX), y))
 
     def b_x_wait(dx):
-        arrive(chunk(oc, -dx, 0), b_send.at[dx - 1], b_recv.at[dx - 1], at(dx=NX - dx))
+        arrive(chunk(oc, -dx, 0), b_send.at[dx], b_recv.at[dx], partner)
 
     def b_reach(dx, dirn):
         return (4 if dirn > 0 else 3) if dx % 2 == 0 else (3 if dirn > 0 else 4)
 
     def b_idx(dx, dirn, s):
-        return 3 + dx * 8 + (s - 1 if dirn > 0 else 3 + s)
+        return 4 + dx * 8 + (s - 1 if dirn > 0 else 3 + s)
 
     def b_y(dx, dirn, s):
         k = chunk(oc, -dx, -dirn * (s - 1))
@@ -147,19 +161,15 @@
     a_x(0, 1)
     a_x(0, -1)
 
-    arrive(ct.at[oc, x, y], pr_send.at[0], pr_recv.at[0], partner)
-    for dx in (1, 3, 2):
+    for dx in (0, 1, 3, 2):
         b_x(dx)
+    tell(1)
+    b_x_wait(0)
     b_y(0, 1, 1)
     b_y(0, -1, 1)
-    load_x.wait()
     send(xb.at[c], xb.at[c], pr_send.at[1], pr_recv.at[1], partner)
     send(fb_hbm.at[oc, 0], fb.at[c], pr_send.at[2], pr_recv.at[2], partner)
 
-    def y_of(j):
-        return j
-
-    a_x_done = []
     for s in range(1, 5):
         a_y_wait(1, s)
         if s < 4:
@@ -183,26 +193,28 @@
                     b_y_wait(dx, dirn, s)
                     if s < b_reach(dx, dirn):
                         b_y(dx, dirn, s + 1)
+        told(s)
+        tell(s + 1)
         ready = {1: (0,), 2: (1, 7), 3: (2, 6), 4: (3, 5)}[s]
         for j in ready:
             d = far_dir(j)
             a_x_wait(j, d)
             a_x_far(j)
             a_x_wait(j, -d)
-            a_x_done.append(j)
     d = far_dir(4)
     a_x_wait(4, d)
     a_x_far(4)
     a_x_wait(4, -d)
+    told(5)
+    arrive(xb.at[oc], pr_send.at[1], pr_recv.at[1], partner)
+    arrive(fb.at[oc], pr_send.at[2], pr_recv.at[2], partner)
+    load_f.wait()
+    load_q.wait()
+    x_own = xb[c].astype(jnp.float32).T.astype(jnp.bfloat16)
+    x_oth = xb[oc].astype(jnp.float32).T.astype(jnp.bfloat16)
     for j in (0, 1, 7, 2, 6, 3, 5, 4):
         a_x_far_wait(j)
 
-    load_f.wait()
-    arrive(xb.at[oc], pr_send.at[1], pr_recv.at[1], partner)
-    arrive(fb.at[oc], pr_send.at[2], pr_recv.at[2], partner)
-    x_own = xb[c].astype(jnp.float32).T.astype(jnp.bfloat16)
-    x_oth = xb[oc].astype(jnp.float32).T.astype(jnp.bfloat16)
-    load_q.wait()
     width = lax.broadcasted_iota(jnp.int32, (1, 128), 1)
     rank = ranks[c]
     live = width < rank
@@ -211,11 +223,10 @@
         cols = pl.ds(b * 256, 256)
         own = fb[c, :, cols] + nt(x_own, ct[c, b].reshape(256, 512), None)
         oth = fb[oc, :, cols] + nt(x_oth, ct[oc, b].reshape(256, 512), None)
-        g_out[c, :, cols] = own
+        gw[:, cols] = own
         gx[:, cols] = oth
         both = own + oth
-        total = total + nn(both, jnp.where(live, qv[cols, :], 0.0))
-        cf_t[cols, :] = both.T
+        total = total + three(nn, split(both), split(jnp.where(live, qv[cols, :], 0.0)))
     for i in range(NZ):
         lo, hi = i * PIECE, min((i + 1) * PIECE, 256)
         if hi - lo == PIECE:
@@ -229,6 +240,11 @@
     for d in ZOFFS:
         send(pp.at[lax.rem(z + d, NZ)], rs.at[d], z_send.at[d], z_recv.at[d], at(dz=d))
     send(gx, g_out.at[c], pr_send.at[3], pr_recv.at[3], partner)
+    keep_g = pltpu.make_async_copy(gw, g_out.at[c], l_sem.at[4])
+    keep_g.start()
+    for b in range(NX):
+        cols = pl.ds(b * 256, 256)
+        cf_h[cols, :], cf_l[cols, :] = split((gw[:, cols] + gx[:, cols]).T)
     acc = pp[z]
     for d in reversed(ZOFFS):
         arrive(rs.at[d], z_send.at[d], z_recv.at[d], at(dz=NZ - d))
@@ -249,9 +265,10 @@
     for n, (dx, dy) in enumerate(OFFS):
         to = lax.rem(x + dx, NX) * NY + lax.rem(y + dy, NY)
         send(gl.at[to], g_rs.at[n], f_send.at[n], f_recv.at[n], at(dx=dx, dy=dy))
+    left_parts = split(left)
     for b in range(NX):
         rows = pl.ds(b * 256, 256)
-        s_src[pl.ds(b * NY, NY)] = nn(cf_t[rows, :], left).reshape(NY, 32, 128)
+        s_src[pl.ds(b * NY, NY)] = three(nn, (cf_h[rows, :], cf_l[rows, :]), left_parts).reshape(NY, 32, 128)
     for n, (dx, dy) in enumerate(OFFS):
         to = lax.rem(x + dx, NX) * NY + lax.rem(y + dy, NY)
         send(s_src.at[to], s_rs.at[n], f_send.at[32 + n], f_recv.at[32 + n], at(dx=dx, dy=dy))
@@ -304,6 +321,10 @@
     for i in range(1, NZ):
         acc = acc + s_z[i]
     s_out[c, f] = acc
+
+    def forward(k, i):
+        send(s_out.at[c, k], s_out.at[c, k], f_send.at[128 + i], f_recv.at[128 + i], partner)
+
     for n, (dx, dy) in enumerate(OFFS):
         send(s_out.at[c, f], s_out.at[c, f], f_send.at[96 + n], f_recv.at[96 + n], at(dx=dx, dy=dy))
 
@@ -314,27 +335,35 @@
     li_out[c] = unit * (1.0 / jnp.sqrt(diag))
     send(li_out.at[c], li_out.at[c], pr_send.at[5], pr_recv.at[5], partner)
 
+    forward(f, NF - 1)
     for n, (dx, dy) in reversed(list(enumerate(OFFS))):
-        sx, sy = lax.rem(x + NX - dx, NX), lax.rem(y + NY - dy, NY)
-        arrive(s_out.at[c, sx * NY + sy], f_send.at[96 + n], f_recv.at[96 + n], src(dx, dy))
-    send(s_out.at[c], s_out.at[c], pr_send.at[6], pr_recv.at[6], partner)
+        k = lax.rem(x + NX - dx, NX) * NY + lax.rem(y + NY - dy, NY)
+        arrive(s_out.at[c, k], f_send.at[96 + n], f_recv.at[96 + n], src(dx, dy))
+        forward(k, n)
+    keep_g.wait()
     arrive(g_out.at[oc], pr_send.at[3], pr_recv.at[3], partner)
     arrive(pf_out.at[oc], pr_send.at[4], pr_recv.at[4], partner)
     arrive(li_out.at[oc], pr_send.at[5], pr_recv.at[5], partner)
-    arrive(s_out.at[oc], pr_send.at[6], pr_recv.at[6], partner)
+    arrive(s_out.at[oc, f], f_send.at[128 + NF - 1], f_recv.at[128 + NF - 1], partner)
+    for n, (dx, dy) in reversed(list(enumerate(OFFS))):
+        k = lax.rem(x + NX - dx, NX) * NY + lax.rem(y + NY - dy, NY)
+        arrive(s_out.at[oc, k], f_send.at[128 + n], f_recv.at[128 + n], partner)
     for cp in pending:
         cp.wait_send()
 
 
-def final_kernel(g, s, pf, li, p_out, q_out, e_out):
-    inv = li[0]
-    left = nt(pf[0], inv)
-    p_out[0] = left
-    for b in range(4):
-        rows = pl.ds(b * 256, 256)
-        right = nt(s[0, rows, :], inv)
-        q_out[0, rows, :] = right
-        e_out[0, 0, :, rows] = g[0, :, rows] - nt(left, right)
+def final_kernel(g, s, pf, li, p_out, q_out, e_out, left_h, left_l):
+    inv = split(li[0])
+
+    @pl.when(pl.program_id(1) == 0)
+    def _():
+        left = three(nt, split(pf[0]), inv)
+        p_out[0] = left
+        left_h[...], left_l[...] = split(left)
+
+    right = three(nt, split(s[0]), inv)
+    q_out[0] = right
+    e_out[0, 0] = g[0] - three(nt, (left_h[...], left_l[...]), split(right))
 
 
 def local(inputs, cotangent, feedback, q_init, factor_ranks):
@@ -351,16 +380,16 @@
             jax.ShapeDtypeStruct((2, 128, 128), f32),
         ),
         in_specs=[pl.BlockSpec(memory_space=pltpu.SMEM)] + [anyspace] * 4,
-        out_specs=(vm,) * 4,
+        out_specs=(anyspace, vm, vm, vm),
         scratch_shapes=[
             pltpu.VMEM((2, 512, 256), b16),
-            pltpu.VMEM((2, 512, 32), b16),
-            pltpu.VMEM((32, 512), b16),
             pltpu.VMEM((2, NX, NY, 32, 512), b16),
             pltpu.VMEM((2, 256, 1024), f32),
             pltpu.VMEM((1024, 128), f32),
             pltpu.VMEM((256, 1024), f32),
-            pltpu.VMEM((1024, 256), f32),
+            pltpu.VMEM((256, 1024), f32),
+            pltpu.VMEM((1024, 256), b16),
+            pltpu.VMEM((1024, 256), b16),
             pltpu.VMEM((NZ, PIECE, 128), f32),
             pltpu.VMEM((NZ, PIECE, 128), f32),
             pltpu.VMEM((NZ, PIECE, 128), f32),
@@ -371,34 +400,41 @@
             pltpu.VMEM((NF, 4, 128), f32),
             pltpu.VMEM((NF, 4, 128), f32),
             pltpu.VMEM((128, 128), f32),
-            dma((4,)),
+            dma((5,)),
             dma((7,)), dma((7,)),
             dma((32,)), dma((32,)),
-            dma((35,)), dma((35,)),
             dma((36,)), dma((36,)),
-            dma((128,)), dma((128,)),
+            dma((36,)), dma((36,)),
+            dma((160,)), dma((160,)),
+            pltpu.SemaphoreType.REGULAR((5, 2)),
         ],
         compiler_params=pltpu.CompilerParams(
             collective_id=0, has_side_effects=True, vmem_limit_bytes=56 << 20
         ),
         name="exchange",
-    )(factor_ranks, inputs, cotangent, feedback, q_init)
+    )(factor_ranks, inputs, jnp.swapaxes(cotangent, 1, 2), feedback, q_init)
     s = s.reshape(2, 1024, 128)
 
     def whole(*shape):
-        return pl.BlockSpec((1, *shape), lambda m: (m,) + (0,) * len(shape))
-
+        return pl.BlockSpec((1, *shape), lambda m, b: (m,) + (0,) * len(shape))
+
+    blocks = 4
+    width = 1024 // blocks
+    rows = pl.BlockSpec((1, width, 128), lambda m, b: (m, b, 0))
     return pl.pallas_call(
         final_kernel,
-        grid=(2,),
+        grid=(2, blocks),
         out_shape=(
             jax.ShapeDtypeStruct((2, 256, 128), f32),
             jax.ShapeDtypeStruct((2, 1024, 128), f32),
             jax.ShapeDtypeStruct((2, 1, 256, 1024), f32),
         ),
-        in_specs=[whole(256, 1024), whole(1024, 128), whole(256, 128), whole(128, 128)],
-        out_specs=(whole(256, 128), whole(1024, 128), whole(1, 256, 1024)),
-        compiler_params=pltpu.CompilerParams(dimension_semantics=("arbitrary",)),
+        in_specs=[
+            pl.BlockSpec((1, 256, width), lambda m, b: (m, 0, b)), rows, whole(256, 128), whole(128, 128),
+        ],
+        out_specs=(whole(256, 128), rows, pl.BlockSpec((1, 1, 256, width), lambda m, b: (m, 0, 0, b))),
+        scratch_shapes=[pltpu.VMEM((256, 128), b16)] * 2,
+        compiler_params=pltpu.CompilerParams(dimension_semantics=("arbitrary", "arbitrary")),
         name="finish",
     )(g, s, pf, li)
 

time: 110 us -> 106 us (0.964)
  Pallas kernels: 107 us -> 105 us
  local copies, waits for them, and re-layouts: 1.68 us -> 0 us
    pallas_call x1, Pallas kernels: 101 us -> 96.9 us  [local(): pl.pallas_call(comm_kernel, out_shape=(jax.ShapeDtypeStruct((2, 256, 1024...]
    pallas_call x1, Pallas kernels: 6.03 us -> 8.53 us  [local(): pl.pallas_call(final_kernel, grid=(2, blocks), out_shape=(jax.ShapeDtypeS...]
    unnamed x1 -> x0, local copies, waits for them, and re-layouts: 1.68 us -> none
where the time goes in v2:
time: 106 us
  Pallas kernels  105 us (99%)
    pallas_call x1, Pallas kernels, local(): pl.pallas_call(comm_kernel, out_shape=(jax.ShapeDtypeStruct((2, 256, 1024...  96.9 us
    pallas_call x1, Pallas kernels, local(): pl.pallas_call(final_kernel, grid=(2, blocks), out_shape=(jax.ShapeDtypeS...  8.53 us

profile of v2, /device:TPU:1, one launch (start us, length us, event | category | flops | bytes accessed | tf_op | source)
XLA Modules:
  0.0 106.0 jit_solution(16125962499465050304)
XLA Ops:
  0.6 96.9 %exchange.1 = (f32[2,256,1024]{2,1,0:T(8,128)}, f32[2,32,32,128]{3,2,1,0:T(8,128)}, f32[2,256,128]{2,1,0:T(8,128)}, f32[2,128,128]{2,1,0:T(8,128)}) custom-call(s32[2]{0:T(128)} %ranks.1, bf16[512,256]{1,0:T(8,128)(2,1)} %x_hbm.1, bf16[2,32,512]{2,1,0:T(8,128)(2,1)} %bitcast.3, f32[2,1,256,1024]{3,2,1,0:T(8,128)} %fb_hbm.1, f32[2,1024,128]{2,1,0:T(8,128)} %q_hbm.1), custom_call_target="tpu_custom_call" | custom-call | tf_op jit(solution)/shard_map/exchange/pallas_call | solution.py:374
  97.5 8.5 %finish.1 = (f32[2,256,128]{2,1,0:T(8,128)}, f32[2,1024,128]{2,1,0:T(8,128)}, f32[2,1,256,1024]{3,2,1,0:T(8,128)}) custom-call(f32[2,256,1024]{2,1,0:T(8,128)} %get-tuple-element.7.g, f32[2,1024,128]{2,1,0:T(8,128)} %bitcast.2, f32[2,256,128]{2,1,0:T(8,128)} %get-tuple-element.9.pf, f32[2,128,128]{2,1,0:T(8,128)} %get-tuple-element.10.li), custom_call_target="tpu_custom_call" | custom-call | tf_op jit(solution)/shard_map/finish/pallas_call | solution.py:424

commit v3 on v2

v3 whole, which is shorter than its diff:
```python
import functools

import jax
import jax.numpy as jnp
from jax import lax
from jax.experimental import pallas as pl
from jax.experimental.pallas import tpu as pltpu
from jax.sharding import Mesh
from jax.sharding import PartitionSpec as P

MESH = pl.DeviceIdType.MESH
HI = lax.Precision.HIGHEST
NZ, NX, NY = 12, 4, 8
NF = NX * NY
STEPS = (48, 80)
PIECE = 24
DP = ("z", "c")
FS = ("x", "y")

OFFS = sorted(
    [(dx, dy) for dx in range(NX) for dy in range(NY) if dx or dy],
    key=lambda o: -(min(o[0], NX - o[0]) + min(o[1], NY - o[1])),
)
YOFFS = (4, 3, 5, 2, 6, 1, 7)
ZOFFS = sorted(range(1, NZ), key=lambda d: -min(d, NZ - d))


def nt(a, b, precision=HI):
    return lax.dot_general(
        a, b, (((1,), (1,)), ((), ())), precision=precision, preferred_element_type=jnp.float32
    )


def nn(a, b, precision=HI):
    return lax.dot_general(
        a, b, (((1,), (0,)), ((), ())), precision=precision, preferred_element_type=jnp.float32
    )


def split(a):
    high = a.astype(jnp.bfloat16)
    return high, (a - high.astype(jnp.float32)).astype(jnp.bfloat16)


def three(dot, a, b):
    (ah, al), (bh, bl) = a, b
    return dot(ah, bh, None) + (dot(ah, bl, None) + dot(al, bh, None))


def comm_kernel(
    ranks, x_hbm, cot_hbm, fb_hbm, q_hbm,
    g_out, s_out, p_out, r_out, li_out,
    xb, ct, fb, qv, gx, cf_h, cf_l, pp, pq, pr, rs, pf3, pf_x, s_src, s_rs, s_t, s_z, gl, g_rs, gg, mat,
    l_sem, pr_send, pr_recv, a_send, a_recv, b_send, b_recv, z_send, z_recv, f_send, f_recv, near,
):
    z, c, x, y = (lax.axis_index(n) for n in ("z", "c", "x", "y"))
    oc = 1 - c
    f = x * NY + y
    pending = []

    def at(dz=0, dx=0, dy=0):
        return (lax.rem(z + dz, NZ), c, lax.rem(x + dx, NX), lax.rem(y + dy, NY))

    partner = (z, oc, x, y)

    def send(src, dst, ssem, rsem, dev):
        cp = pltpu.make_async_remote_copy(
            src_ref=src, dst_ref=dst, send_sem=ssem, recv_sem=rsem, device_id=dev, device_id_type=MESH
        )
        cp.start()
        pending.append(cp)

    def arrive(dst, ssem, rsem, dev):
        pltpu.make_async_remote_copy(
            src_ref=dst, dst_ref=dst, send_sem=ssem, recv_sem=rsem, device_id=dev, device_id_type=MESH
        ).wait_recv()

    barrier = pltpu.get_barrier_semaphore()
    peers = [partner] + [at(dx=dx) for dx in (1, 2, 3)]
    peers += [at(dy=1), at(dy=NY - 1), at(dz=1), at(dz=NZ - 1)]
    for peer in peers:
        pl.semaphore_signal(barrier, inc=1, device_id=peer, device_id_type=MESH)

    loads = [
        pltpu.make_async_copy(src, dst, l_sem.at[i])
        for i, (src, dst) in enumerate(
            [(cot_hbm.at[r], ct.at[r, x, y]) for r in range(2)] + [(x_hbm, xb), (fb_hbm, fb), (q_hbm, qv)]
        )
    ]
    for cp in loads:
        cp.start()
    for cp in loads[:2]:
        cp.wait()

    pl.semaphore_wait(barrier, len(peers))

    def tell(r):
        for n, dz in enumerate((1, NZ - 1)):
            pl.semaphore_signal(near.at[r - 1, n], inc=1, device_id=at(dz=dz), device_id_type=MESH)

    def told(r):
        for n in range(2):
            pl.semaphore_wait(near.at[r - 1, n], 1)

    def chunk(r, dx, dy):
        return ct.at[r, lax.rem(x + dx + NX, NX), lax.rem(y + dy + NY, NY)]

    def a_y(dirn, s):
        k = chunk(0, 0, -dirn * (s - 1))
        i = (s - 1) if dirn > 0 else 3 + s
        send(k, k, a_send.at[i], a_recv.at[i], at(dy=dirn % NY))

    def a_y_wait(dirn, s):
        i = (s - 1) if dirn > 0 else 3 + s
        arrive(chunk(0, 0, -dirn * s), a_send.at[i], a_recv.at[i], at(dy=-dirn % NY))

    def a_x(j, dirn):
        k = chunk(0, 0, -j)
        i = 8 + j * 3 + (0 if dirn > 0 else 1)
        send(k, k, a_send.at[i], a_recv.at[i], at(dx=dirn % NX))

    def a_x_wait(j, dirn):
        i = 8 + j * 3 + (0 if dirn > 0 else 1)
        arrive(chunk(0, -dirn, -j), a_send.at[i], a_recv.at[i], at(dx=-dirn % NX))

    def far_dir(j):
        return 1 if j % 2 == 0 else -1

    def a_x_far(j):
        d = far_dir(j)
        k = chunk(0, -d, -j)
        i = 8 + j * 3 + 2
        send(k, k, a_send.at[i], a_recv.at[i], at(dx=d % NX))

    def a_x_far_wait(j):
        d = far_dir(j)
        i = 8 + j * 3 + 2
        arrive(chunk(0, -2 * d, -j), a_send.at[i], a_recv.at[i], at(dx=-d % NX))

    def b_x(dx):
        k = chunk(1, 0, 0)
        send(k, k, b_send.at[dx], b_recv.at[dx], at(dx=dx))

    def b_x_wait(dx):
        arrive(chunk(1, -dx, 0), b_send.at[dx], b_recv.at[dx], at(dx=NX - dx))

    def b_reach(dx, dirn):
        return (4 if dirn > 0 else 3) if dx % 2 == 0 else (3 if dirn > 0 else 4)

    def b_idx(dx, dirn, s):
        return 4 + dx * 8 + (s - 1 if dirn > 0 else 3 + s)

    def b_y(dx, dirn, s):
        k = chunk(1, -dx, -dirn * (s - 1))
        i = b_idx(dx, dirn, s)
        send(k, k, b_send.at[i], b_recv.at[i], at(dy=dirn % NY))

    def b_y_wait(dx, dirn, s):
        i = b_idx(dx, dirn, s)
        arrive(chunk(1, -dx, -dirn * s), b_send.at[i], b_recv.at[i], at(dy=-dirn % NY))

    a_y(1, 1)
    a_y(-1, 1)
    a_x(0, 1)
    a_x(0, -1)

    for dx in (1, 3, 2):
        b_x(dx)
    b_y(0, 1, 1)
    b_y(0, -1, 1)
    tell(1)

    for s in range(1, 5):
        a_y_wait(1, s)
        if s < 4:
            a_y(1, s + 1)
        a_x(s, 1)
        a_x(s, -1)
        if s < 4:
            a_y_wait(-1, s)
            if s < 3:
                a_y(-1, s + 1)
            a_x(NY - s, 1)
            a_x(NY - s, -1)
        if s == 1:
            for dx in (1, 3, 2):
                b_x_wait(dx)
                b_y(dx, 1, 1)
                b_y(dx, -1, 1)
        for dx in (0, 1, 3, 2):
            for dirn in (1, -1):
                if s <= b_reach(dx, dirn):
                    b_y_wait(dx, dirn, s)
                    if s < b_reach(dx, dirn):
                        b_y(dx, dirn, s + 1)
        told(s)
        tell(s + 1)
        ready = {1: (0,), 2: (1, 7), 3: (2, 6), 4: (3, 5)}[s]
        for j in ready:
            d = far_dir(j)
            a_x_wait(j, d)
            a_x_far(j)
            a_x_wait(j, -d)
    d = far_dir(4)
    a_x_wait(4, d)
    a_x_far(4)
    a_x_wait(4, -d)
    told(5)
    for cp in loads[2:]:
        cp.wait()
    x_t = xb[...].astype(jnp.float32).T.astype(jnp.bfloat16)
    for j in (0, 1, 7, 2, 6, 3, 5, 4):
        a_x_far_wait(j)

    width = lax.broadcasted_iota(jnp.int32, (1, 128), 1)
    rank = ranks[c]
    for m, out in ((oc, pq), (c, pp)):
        live = width < ranks[m]
        total = jnp.zeros((256, 128), jnp.float32)
        for b in range(NX):
            cols = pl.ds(b * 256, 256)
            full = fb[m, 0, :, cols] + nt(x_t, ct[m, b].reshape(256, 512), None)
            g_out[m, :, cols] = full
            total = total + three(nn, split(full), split(jnp.where(live, qv[m, cols, :], 0.0)))
        for i in range(NZ):
            lo, hi = i * PIECE, min((i + 1) * PIECE, 256)
            if hi - lo == PIECE:
                out[i] = total[lo:hi]
            elif hi > lo:
                out[i, : hi - lo] = total[lo:hi]
                out[i, hi - lo :] = jnp.zeros((PIECE - (hi - lo), 128), jnp.float32)
            else:
                out[i] = jnp.zeros((PIECE, 128), jnp.float32)
        if out is pq:
            send(pq, pr, pr_send.at[0], pr_recv.at[0], partner)
    arrive(pr, pr_send.at[0], pr_recv.at[0], partner)
    pp[...] = pp[...] + pr[...]

    for d in ZOFFS:
        send(pp.at[lax.rem(z + d, NZ)], rs.at[d], z_send.at[d], z_recv.at[d], at(dz=d))
    for b in range(4):
        rows = pl.ds(b * 64, 64)
        send(g_out.at[oc, rows], gx.at[rows], pr_send.at[1 + b], pr_recv.at[1 + b], partner)
    acc = pp[z]
    for d in reversed(ZOFFS):
        arrive(rs.at[d], z_send.at[d], z_recv.at[d], at(dz=NZ - d))
        acc = acc + rs[d]
    pf3[z] = acc
    for d in ZOFFS:
        send(pf3.at[z], pf3.at[z], z_send.at[12 + d], z_recv.at[12 + d], at(dz=d))
    for b in range(4):
        rows = pl.ds(b * 64, 64)
        arrive(gx.at[rows], pr_send.at[1 + b], pr_recv.at[1 + b], partner)
    for b in range(NX):
        cols = pl.ds(b * 256, 256)
        cf_h[cols, :], cf_l[cols, :] = split((g_out[c, :, cols] + gx[:, cols]).T)
    for d in reversed(ZOFFS):
        zs = lax.rem(z + NZ - d, NZ)
        arrive(pf3.at[zs], z_send.at[12 + d], z_recv.at[12 + d], at(dz=NZ - d))
    left = pf3[...].reshape(NZ * PIECE, 128)[:256]

    gram = nn(left.T, left)
    for i in range(NF):
        gl[i] = gram[4 * i : 4 * i + 4]
    for n, (dx, dy) in enumerate(OFFS):
        to = lax.rem(x + dx, NX) * NY + lax.rem(y + dy, NY)
        send(gl.at[to], g_rs.at[n], f_send.at[n], f_recv.at[n], at(dx=dx, dy=dy))
    left_parts = split(left)
    for b in range(NX):
        rows = pl.ds(b * 256, 256)
        s_src[pl.ds(b * NY, NY)] = three(nn, (cf_h[rows, :], cf_l[rows, :]), left_parts).reshape(NY, 32, 128)
    for dy in YOFFS + (0,):
        for dx in (2, 1, 3):
            to = lax.rem(x + dx, NX) * NY + lax.rem(y + dy, NY)
            i = dx * NY + dy
            send(s_src.at[to], s_rs.at[i], f_send.at[32 + i], f_recv.at[32 + i], at(dx=dx))

    send(pf3, pf_x, pr_send.at[5], pr_recv.at[5], partner)

    def src(dx, dy):
        return at(dx=(NX - dx) % NX, dy=(NY - dy) % NY)

    def gram_owner():
        acc = gl[f]
        for n, (dx, dy) in reversed(list(enumerate(OFFS))):
            arrive(g_rs.at[n], f_send.at[n], f_recv.at[n], src(dx, dy))
            acc = acc + g_rs[n]
        gg[f] = acc
        for n, (dx, dy) in enumerate(OFFS):
            send(gg.at[f], gg.at[f], f_send.at[64 + n], f_recv.at[64 + n], at(dx=dx, dy=dy))

    for dy in YOFFS + (0,):
        if dy == 2:
            gram_owner()
        acc = s_src[x * NY + lax.rem(y + dy, NY)]
        for dx in (1, 3, 2):
            i = dx * NY + dy
            arrive(s_rs.at[i], f_send.at[32 + i], f_recv.at[32 + i], at(dx=NX - dx))
            acc = acc + s_rs[i]
        if dy:
            s_t[dy] = acc
            send(s_t.at[dy], s_rs.at[dy], f_send.at[32 + dy], f_recv.at[32 + dy], at(dy=dy))
    for dy in reversed(YOFFS):
        arrive(s_rs.at[dy], f_send.at[32 + dy], f_recv.at[32 + dy], at(dy=NY - dy))
        acc = acc + s_rs[dy]
    s_z[z] = acc
    for d in ZOFFS:
        send(s_z.at[z], s_z.at[z], z_send.at[24 + d], z_recv.at[24 + d], at(dz=d))

    for n, (dx, dy) in reversed(list(enumerate(OFFS))):
        sx, sy = lax.rem(x + NX - dx, NX), lax.rem(y + NY - dy, NY)
        arrive(gg.at[sx * NY + sy], f_send.at[64 + n], f_recv.at[64 + n], src(dx, dy))
    for i in range(NF):
        mat[4 * i : 4 * i + 4, :] = gg[i]
    row_id = lax.broadcasted_iota(jnp.int32, (128, 128), 0)
    col_id = lax.broadcasted_iota(jnp.int32, (128, 128), 1)
    mat[...] = mat[...] + jnp.where((row_id == col_id) & (col_id >= rank), 1.0, 0.0)

    def eliminate(j, carry):
        m = mat[...]
        row = mat[pl.ds(j, 1), :]
        hit = col_id == j
        hit1 = width == j
        pivot = jnp.sum(jnp.where(hit1, row, 0.0), axis=1, keepdims=True)
        col = jnp.sum(jnp.where(hit, m, 0.0), axis=1, keepdims=True)
        factor = jnp.where(row_id > j, col / pivot, 0.0)
        mat[...] = jnp.where(hit & (row_id > j), 0.0, m) - factor * jnp.where(hit1, 1.0, row)
        return carry

    lax.fori_loop(0, STEPS[0], eliminate, 0)

    for d in reversed(ZOFFS):
        zs = lax.rem(z + NZ - d, NZ)
        arrive(s_z.at[zs], z_send.at[24 + d], z_recv.at[24 + d], at(dz=NZ - d))
    acc = s_z[0]
    for i in range(1, NZ):
        acc = acc + s_z[i]
    s_out[c, f] = acc

    def piece(dx, dy):
        return lax.rem(x + NX - dx, NX) * NY + lax.rem(y + NY - dy, NY)

    def forward(dx, dy):
        k, i = piece(dx, dy), 128 + dx * NY + dy
        send(s_out.at[c, k], s_out.at[c, k], f_send.at[i], f_recv.at[i], partner)

    def spread(dy):
        k = piece(0, dy)
        for dx in (2, 1, 3):
            i = 96 + dx * NY + dy
            send(s_out.at[c, k], s_out.at[c, k], f_send.at[i], f_recv.at[i], at(dx=dx))
        forward(0, dy)

    for dy in YOFFS:
        send(s_out.at[c, f], s_out.at[c, f], f_send.at[96 + dy], f_recv.at[96 + dy], at(dy=dy))
    spread(0)
    lax.fori_loop(STEPS[0], STEPS[1], eliminate, 0)
    for dy in reversed(YOFFS):
        arrive(s_out.at[c, piece(0, dy)], f_send.at[96 + dy], f_recv.at[96 + dy], at(dy=NY - dy))
        spread(dy)

    lax.fori_loop(STEPS[1], 128, eliminate, 0)
    m = mat[...]
    diag = jnp.sum(jnp.where(row_id == col_id, m, 0.0), axis=1, keepdims=True)
    unit = jnp.where(row_id == col_id, 1.0, jnp.where(row_id > col_id, m, 0.0))
    li_out[c] = unit * (1.0 / jnp.sqrt(diag))
    send(li_out.at[c], li_out.at[c], pr_send.at[6], pr_recv.at[6], partner)

    def factor(m, parts):
        inv = split(li_out[m])
        own = three(nt, parts, inv)
        p_out[m] = own
        r_out[m] = three(nn, split(own), inv)

    factor(c, left_parts)
    for dy in (0,) + YOFFS[::-1]:
        for dx in (1, 3, 2):
            i = 96 + dx * NY + dy
            arrive(s_out.at[c, piece(dx, dy)], f_send.at[i], f_recv.at[i], at(dx=NX - dx))
            forward(dx, dy)
    arrive(pf_x, pr_send.at[5], pr_recv.at[5], partner)
    arrive(li_out.at[oc], pr_send.at[6], pr_recv.at[6], partner)
    factor(oc, split(pf_x[...].reshape(NZ * PIECE, 128)[:256]))
    for dy in (0,) + YOFFS[::-1]:
        for dx in range(NX):
            i = 128 + dx * NY + dy
            arrive(s_out.at[oc, piece(dx, dy)], f_send.at[i], f_recv.at[i], partner)
    for cp in pending:
        cp.wait_send()


def final_kernel(g, s, p, r, li, p_out, q_out, e_out, q_buf, e_buf, sem):
    puts = []

    def put(src, dst):
        puts.append(pltpu.make_async_copy(src, dst, sem.at[len(puts)]))
        puts[-1].start()

    put(p, p_out)
    for m in range(2):
        inv, right = split(li[m]), split(r[m])
        for b in range(NX):
            cols = pl.ds(b * 256, 256)
            raw = split(s[m, b * NY : (b + 1) * NY].reshape(256, 128))
            e_buf[m, :, cols] = g[m, :, cols] - three(nt, right, raw)
            put(e_buf.at[m, :, cols], e_out.at[m, 0, :, cols])
            q_buf[m, cols, :] = three(nt, raw, inv)
            put(q_buf.at[m, cols, :], q_out.at[m, cols, :])
    for cp in puts:
        cp.wait()


def local(inputs, cotangent, feedback, q_init, factor_ranks):
    f32, b16 = jnp.float32, jnp.bfloat16
    vm = pl.BlockSpec(memory_space=pltpu.VMEM)
    anyspace = pl.BlockSpec(memory_space=pl.ANY)
    dma = pltpu.SemaphoreType.DMA
    parts = pl.pallas_call(
        comm_kernel,
        out_shape=(
            pltpu.VMEM((2, 256, 1024), f32),
            pltpu.VMEM((2, NF, 32, 128), f32),
            pltpu.VMEM((2, 256, 128), f32),
            pltpu.VMEM((2, 256, 128), f32),
            pltpu.VMEM((2, 128, 128), f32),
        ),
        in_specs=[pl.BlockSpec(memory_space=pltpu.SMEM)] + [anyspace] * 4,
        out_specs=(vm,) * 5,
        scratch_shapes=[
            pltpu.VMEM((512, 256), b16),
            pltpu.VMEM((2, NX, NY, 32, 512), b16),
            pltpu.VMEM((2, 1, 256, 1024), f32),
            pltpu.VMEM((2, 1024, 128), f32),
            pltpu.VMEM((256, 1024), f32),
            pltpu.VMEM((1024, 256), b16),
            pltpu.VMEM((1024, 256), b16),
            pltpu.VMEM((NZ, PIECE, 128), f32),
            pltpu.VMEM((NZ, PIECE, 128), f32),
            pltpu.VMEM((NZ, PIECE, 128), f32),
            pltpu.VMEM((NZ, PIECE, 128), f32),
            pltpu.VMEM((NZ, PIECE, 128), f32),
            pltpu.VMEM((NZ, PIECE, 128), f32),
            pltpu.VMEM((NF, 32, 128), f32),
            pltpu.VMEM((NF, 32, 128), f32),
            pltpu.VMEM((NY, 32, 128), f32),
            pltpu.VMEM((NZ, 32, 128), f32),
            pltpu.VMEM((NF, 4, 128), f32),
            pltpu.VMEM((NF, 4, 128), f32),
            pltpu.VMEM((NF, 4, 128), f32),
            pltpu.VMEM((128, 128), f32),
            dma((5,)),
            dma((7,)), dma((7,)),
            dma((32,)), dma((32,)),
            dma((36,)), dma((36,)),
            dma((36,)), dma((36,)),
            dma((160,)), dma((160,)),
            pltpu.SemaphoreType.REGULAR((5, 2)),
        ],
        compiler_params=pltpu.CompilerParams(
            collective_id=0, has_side_effects=True, vmem_limit_bytes=32 << 20
        ),
        name="exchange",
    )(factor_ranks, inputs, jnp.swapaxes(cotangent, 1, 2), feedback, q_init)
    return pl.pallas_call(
        final_kernel,
        out_shape=(
            jax.ShapeDtypeStruct((2, 256, 128), f32),
            jax.ShapeDtypeStruct((2, 1024, 128), f32),
            jax.ShapeDtypeStruct((2, 1, 256, 1024), f32),
        ),
        in_specs=[vm] * 5,
        out_specs=(anyspace,) * 3,
        scratch_shapes=[pltpu.VMEM((2, 1024, 128), f32), pltpu.VMEM((2, 256, 1024), f32), dma((17,))],
        compiler_params=pltpu.CompilerParams(vmem_limit_bytes=16 << 20),
        name="finish",
    )(*parts)


def solution(mesh):
    torus = Mesh(mesh.devices.reshape(NZ, 2, NX, NY), ("z", "c", "x", "y"))
    placed = (P(DP, FS), P(None, DP, FS), P(None, DP, FS, None), P(), P())
    return jax.shard_map(
        local,
        mesh=torus,
        in_specs=placed,
        out_specs=(P(None, FS, None), P(), P(None, DP, FS, None)),
        check_vma=False,
    )
```

time: 106 us -> 103 us (0.972)
  Pallas kernels: 105 us -> 96.9 us
  local copies, waits for them, and re-layouts: 0 us -> 5.25 us
    pallas_call x2, Pallas kernels: 105 us -> 96.9 us  [the longest x1 94.6 us: local(): pl.pallas_call(comm_kernel, out_shape=(pltpu.VMEM((2, 256, 1024), f32), p...]
    unnamed x0 -> x10, local copies, waits for them, and re-layouts: none -> 5.25 us
where the time goes in v3:
time: 103 us
  Pallas kernels  96.9 us (94%)
  local copies, waits for them, and re-layouts  5.25 us (5%)
    pallas_call x1, Pallas kernels, local(): pl.pallas_call(comm_kernel, out_shape=(pltpu.VMEM((2, 256, 1024), f32), p...  94.6 us
    unnamed x10, local copies, waits for them, and re-layouts  5.25 us
    pallas_call x1, Pallas kernels, local(): pl.pallas_call(final_kernel, out_shape=(jax.ShapeDtypeStruct((2, 256, 128...  2.32 us

profile of v3, /device:TPU:1, one launch (start us, length us, event | category | flops | bytes accessed | tf_op | source)
XLA Modules:
  0.0 102.8 jit_solution(11765494346393881610)
XLA Ops:
  0.6 0.0 copy-start
  0.6 1.6 %copy-done = f32[2,1,256,1024]{3,2,1,0:T(8,128)S(1)} copy-done((f32[2,1,256,1024]{3,2,1,0:T(8,128)S(1)}, f32[2,1,256,1024]{3,2,1,0:T(8,128)}, u32[]{:S(2)}) %copy-start) | copy-done | bytes 2097176
  2.2 0.0 copy-start.1
  2.2 1.2 %copy-done.1 = f32[2,1024,128]{2,1,0:T(8,128)S(1)} copy-done((f32[2,1024,128]{2,1,0:T(8,128)S(1)}, f32[2,1024,128]{2,1,0:T(8,128)}, u32[]{:S(2)}) %copy-start.1) | copy-done | bytes 1048600
  3.4 0.0 copy-start.2
  3.5 0.9 copy-done.2
  4.4 0.0 copy-start.3
  4.4 0.8 copy-done.3
  5.2 0.0 copy-start.4
  5.2 0.7 copy-done.4
  5.9 94.6 %exchange.1 = (f32[2,256,1024]{2,1,0:T(8,128)S(1)}, f32[2,32,32,128]{3,2,1,0:T(8,128)S(1)}, f32[2,256,128]{2,1,0:T(8,128)S(1)}, f32[2,256,128]{2,1,0:T(8,128)S(1)}, f32[2,128,128]{2,1,0:T(8,128)S(1)}) custom-call(s32[2]{0:T(128)S(1)} %copy-done.4, bf16[512,256]{1,0:T(8,128)(2,1)S(1)} %copy-done.2, bf16[2,32,512]{2,1,0:T(8,128)(2,1)S(1)} %bitcast.1, ...), custom_call_target="tpu_custom_call" | custom-call | tf_op jit(solution)/shard_map/exchange/pallas_call | solution.py:418
  100.5 2.3 %finish.1 = (f32[2,256,128]{2,1,0:T(8,128)}, f32[2,1024,128]{2,1,0:T(8,128)}, f32[2,1,256,1024]{3,2,1,0:T(8,128)}) custom-call(f32[2,256,1024]{2,1,0:T(8,128)S(1)} %get-tuple-element.8.g, f32[2,32,32,128]{3,2,1,0:T(8,128)S(1)} %get-tuple-element.9.s, f32[2,256,128]{2,1,0:T(8,128)S(1)} %get-tuple-element.10.p, f32[2,256,128]{2,1,0:T(8,128)S(1)} %get-tuple-element.11.r, ...), custom_call_target="tpu_custom_call" | custom-call | tf_op jit(solution)/shard_map/finish/pallas_call | solution.py:464
Async XLA Ops:
  0.6 1.6 %copy-start = (f32[2,1,256,1024]{3,2,1,0:T(8,128)S(1)}, f32[2,1,256,1024]{3,2,1,0:T(8,128)}, u32[]{:S(2)}) copy-start(f32[2,1,256,1024]{3,2,1,0:T(8,128)} %fb_hbm.1) | copy-start | bytes 6291460
  2.2 1.2 %copy-start.1 = (f32[2,1024,128]{2,1,0:T(8,128)S(1)}, f32[2,1024,128]{2,1,0:T(8,128)}, u32[]{:S(2)}) copy-start(f32[2,1024,128]{2,1,0:T(8,128)} %q_hbm.1) | copy-start | bytes 3145732
  3.4 0.9 copy-start.2
  4.4 0.8 copy-start.3
  5.2 0.7 copy-start.4

commit v4 on v3

--- a/solution.py
+++ b/solution.py
@@ -70,6 +70,22 @@
         cp.start()
         pending.append(cp)
 
+    def settle(count=None):
+        for cp in pending[:count]:
+            cp.wait_send()
+        del pending[:count]
+
+    def batch(src, dst, sems, k, dev):
+        pltpu.make_async_remote_copy(
+            src_ref=src, dst_ref=dst, send_sem=sems[0].at[k], recv_sem=sems[1].at[k], device_id=dev, device_id_type=MESH
+        ).start()
+
+    def whole(ref, sems, k):
+        return pltpu.make_async_remote_copy(
+            src_ref=ref, dst_ref=ref, send_sem=sems[0].at[k], recv_sem=sems[1].at[k],
+            device_id=partner, device_id_type=MESH,
+        )
+
     def arrive(dst, ssem, rsem, dev):
         pltpu.make_async_remote_copy(
             src_ref=dst, dst_ref=dst, send_sem=ssem, recv_sem=rsem, device_id=dev, device_id_type=MESH
@@ -170,41 +186,44 @@
     b_y(0, -1, 1)
     tell(1)
 
-    for s in range(1, 5):
-        a_y_wait(1, s)
-        if s < 4:
-            a_y(1, s + 1)
-        a_x(s, 1)
-        a_x(s, -1)
-        if s < 4:
-            a_y_wait(-1, s)
-            if s < 3:
-                a_y(-1, s + 1)
-            a_x(NY - s, 1)
-            a_x(NY - s, -1)
-        if s == 1:
-            for dx in (1, 3, 2):
-                b_x_wait(dx)
-                b_y(dx, 1, 1)
-                b_y(dx, -1, 1)
-        for dx in (0, 1, 3, 2):
+    def a_hop(s):
+        for dirn, last in ((1, 4), (-1, 3)):
+            if s <= last:
+                a_y_wait(dirn, s)
+                if s < last:
+                    a_y(dirn, s + 1)
+        for j in (s, NY - s) if s < 4 else (4,):
+            a_x(j, 1)
+            a_x(j, -1)
+
+    def a_far(j):
+        d = far_dir(j)
+        a_x_wait(j, d)
+        a_x_far(j)
+        a_x_wait(j, -d)
+
+    def b_hop(s, dxs):
+        for dx in dxs:
             for dirn in (1, -1):
                 if s <= b_reach(dx, dirn):
                     b_y_wait(dx, dirn, s)
                     if s < b_reach(dx, dirn):
                         b_y(dx, dirn, s + 1)
+
+    a_hop(1)
+    for dx in (1, 3, 2):
+        b_x_wait(dx)
+        b_y(dx, 1, 1)
+        b_y(dx, -1, 1)
+    for s in range(1, 5):
+        b_hop(s, (0,))
         told(s)
         tell(s + 1)
-        ready = {1: (0,), 2: (1, 7), 3: (2, 6), 4: (3, 5)}[s]
-        for j in ready:
-            d = far_dir(j)
-            a_x_wait(j, d)
-            a_x_far(j)
-            a_x_wait(j, -d)
-    d = far_dir(4)
-    a_x_wait(4, d)
-    a_x_far(4)
-    a_x_wait(4, -d)
+        if s < 4:
+            a_hop(s + 1)
+        b_hop(s, (1, 3, 2))
+        for j in {1: (0,), 2: (1, 7), 3: (2, 6), 4: (3, 5, 4)}[s]:
+            a_far(j)
     told(5)
     for cp in loads[2:]:
         cp.wait()
@@ -236,35 +255,42 @@
     arrive(pr, pr_send.at[0], pr_recv.at[0], partner)
     pp[...] = pp[...] + pr[...]
 
+    sent = len(pending)
+    zs_sems = (z_send, z_recv)
     for d in ZOFFS:
-        send(pp.at[lax.rem(z + d, NZ)], rs.at[d], z_send.at[d], z_recv.at[d], at(dz=d))
+        batch(pp.at[lax.rem(z + d, NZ)], rs.at[d], zs_sems, 0, at(dz=d))
     for b in range(4):
         rows = pl.ds(b * 64, 64)
         send(g_out.at[oc, rows], gx.at[rows], pr_send.at[1 + b], pr_recv.at[1 + b], partner)
+    settle(sent)
+    pieces = whole(rs.at[pl.ds(1, NZ - 1)], zs_sems, 0)
+    pieces.wait_recv()
     acc = pp[z]
-    for d in reversed(ZOFFS):
-        arrive(rs.at[d], z_send.at[d], z_recv.at[d], at(dz=NZ - d))
+    for d in range(1, NZ):
         acc = acc + rs[d]
     pf3[z] = acc
     for d in ZOFFS:
-        send(pf3.at[z], pf3.at[z], z_send.at[12 + d], z_recv.at[12 + d], at(dz=d))
+        batch(pf3.at[z], pf3.at[z], zs_sems, 1, at(dz=d))
+    pieces.wait_send()
     for b in range(4):
         rows = pl.ds(b * 64, 64)
         arrive(gx.at[rows], pr_send.at[1 + b], pr_recv.at[1 + b], partner)
     for b in range(NX):
         cols = pl.ds(b * 256, 256)
         cf_h[cols, :], cf_l[cols, :] = split((g_out[c, :, cols] + gx[:, cols]).T)
-    for d in reversed(ZOFFS):
-        zs = lax.rem(z + NZ - d, NZ)
-        arrive(pf3.at[zs], z_send.at[12 + d], z_recv.at[12 + d], at(dz=NZ - d))
+    settle()
+    pieces = whole(pf3.at[pl.ds(0, NZ - 1)], zs_sems, 1)
+    pieces.wait_recv()
+    pieces.wait_send()
     left = pf3[...].reshape(NZ * PIECE, 128)[:256]
 
+    f_sems = (f_send, f_recv)
     gram = nn(left.T, left)
     for i in range(NF):
         gl[i] = gram[4 * i : 4 * i + 4]
     for n, (dx, dy) in enumerate(OFFS):
         to = lax.rem(x + dx, NX) * NY + lax.rem(y + dy, NY)
-        send(gl.at[to], g_rs.at[n], f_send.at[n], f_recv.at[n], at(dx=dx, dy=dy))
+        batch(gl.at[to], g_rs.at[n], f_sems, 0, at(dx=dx, dy=dy))
     left_parts = split(left)
     for b in range(NX):
         rows = pl.ds(b * 256, 256)
@@ -277,17 +303,16 @@
 
     send(pf3, pf_x, pr_send.at[5], pr_recv.at[5], partner)
 
-    def src(dx, dy):
-        return at(dx=(NX - dx) % NX, dy=(NY - dy) % NY)
-
     def gram_owner():
+        pieces = whole(g_rs.at[pl.ds(0, NF - 1)], f_sems, 0)
+        pieces.wait_recv()
         acc = gl[f]
-        for n, (dx, dy) in reversed(list(enumerate(OFFS))):
-            arrive(g_rs.at[n], f_send.at[n], f_recv.at[n], src(dx, dy))
+        for n in range(NF - 1):
             acc = acc + g_rs[n]
         gg[f] = acc
-        for n, (dx, dy) in enumerate(OFFS):
-            send(gg.at[f], gg.at[f], f_send.at[64 + n], f_recv.at[64 + n], at(dx=dx, dy=dy))
+        for dx, dy in OFFS:
+            batch(gg.at[f], gg.at[f], f_sems, 1, at(dx=dx, dy=dy))
+        pieces.wait_send()
 
     for dy in YOFFS + (0,):
         if dy == 2:
@@ -299,17 +324,20 @@
             acc = acc + s_rs[i]
         if dy:
             s_t[dy] = acc
-            send(s_t.at[dy], s_rs.at[dy], f_send.at[32 + dy], f_recv.at[32 + dy], at(dy=dy))
-    for dy in reversed(YOFFS):
-        arrive(s_rs.at[dy], f_send.at[32 + dy], f_recv.at[32 + dy], at(dy=NY - dy))
+            batch(s_t.at[dy], s_rs.at[dy], f_sems, 2, at(dy=dy))
+    settle()
+    pieces = whole(s_rs.at[pl.ds(1, NY - 1)], f_sems, 2)
+    pieces.wait_recv()
+    for dy in range(1, NY):
         acc = acc + s_rs[dy]
     s_z[z] = acc
     for d in ZOFFS:
-        send(s_z.at[z], s_z.at[z], z_send.at[24 + d], z_recv.at[24 + d], at(dz=d))
-
-    for n, (dx, dy) in reversed(list(enumerate(OFFS))):
-        sx, sy = lax.rem(x + NX - dx, NX), lax.rem(y + NY - dy, NY)
-        arrive(gg.at[sx * NY + sy], f_send.at[64 + n], f_recv.at[64 + n], src(dx, dy))
+        batch(s_z.at[z], s_z.at[z], zs_sems, 2, at(dz=d))
+    pieces.wait_send()
+
+    pieces = whole(gg.at[pl.ds(0, NF - 1)], f_sems, 1)
+    pieces.wait_recv()
+    pieces.wait_send()
     for i in range(NF):
         mat[4 * i : 4 * i + 4, :] = gg[i]
     row_id = lax.broadcasted_iota(jnp.int32, (128, 128), 0)
@@ -329,9 +357,9 @@
 
     lax.fori_loop(0, STEPS[0], eliminate, 0)
 
-    for d in reversed(ZOFFS):
-        zs = lax.rem(z + NZ - d, NZ)
-        arrive(s_z.at[zs], z_send.at[24 + d], z_recv.at[24 + d], at(dz=NZ - d))
+    pieces = whole(s_z.at[pl.ds(0, NZ - 1)], zs_sems, 2)
+    pieces.wait_recv()
+    pieces.wait_send()
     acc = s_z[0]
     for i in range(1, NZ):
         acc = acc + s_z[i]
@@ -341,8 +369,8 @@
         return lax.rem(x + NX - dx, NX) * NY + lax.rem(y + NY - dy, NY)
 
     def forward(dx, dy):
-        k, i = piece(dx, dy), 128 + dx * NY + dy
-        send(s_out.at[c, k], s_out.at[c, k], f_send.at[i], f_recv.at[i], partner)
+        k = piece(dx, dy)
+        batch(s_out.at[c, k], s_out.at[c, k], f_sems, 3, partner)
 
     def spread(dy):
         k = piece(0, dy)
@@ -373,6 +401,7 @@
         r_out[m] = three(nn, split(own), inv)
 
     factor(c, left_parts)
+    settle()
     for dy in (0,) + YOFFS[::-1]:
         for dx in (1, 3, 2):
             i = 96 + dx * NY + dy
@@ -381,12 +410,9 @@
     arrive(pf_x, pr_send.at[5], pr_recv.at[5], partner)
     arrive(li_out.at[oc], pr_send.at[6], pr_recv.at[6], partner)
     factor(oc, split(pf_x[...].reshape(NZ * PIECE, 128)[:256]))
-    for dy in (0,) + YOFFS[::-1]:
-        for dx in range(NX):
-            i = 128 + dx * NY + dy
-            arrive(s_out.at[oc, piece(dx, dy)], f_send.at[i], f_recv.at[i], partner)
-    for cp in pending:
-        cp.wait_send()
+    pieces = whole(s_out.at[oc], f_sems, 3)
+    pieces.wait_recv()
+    pieces.wait_send()
 
 
 def final_kernel(g, s, p, r, li, p_out, q_out, e_out, q_buf, e_buf, sem):
@@ -457,7 +483,7 @@
             pltpu.SemaphoreType.REGULAR((5, 2)),
         ],
         compiler_params=pltpu.CompilerParams(
-            collective_id=0, has_side_effects=True, vmem_limit_bytes=32 << 20
+            collective_id=0, has_side_effects=True, vmem_limit_bytes=58 << 20
         ),
         name="exchange",
     )(factor_ranks, inputs, jnp.swapaxes(cotangent, 1, 2), feedback, q_init)

time: 103 us -> 97.7 us (0.949)
  local copies, waits for them, and re-layouts: 5.25 us -> 0 us
    unnamed x10 -> x0, local copies, waits for them, and re-layouts: 5.25 us -> none
where the time goes in v4:
time: 97.7 us; the launch traced here: 97.5 us
  Pallas kernels  96.9 us (99%)
    pallas_call x1, Pallas kernels, local(): pl.pallas_call(comm_kernel, out_shape=(pltpu.VMEM((2, 256, 1024), f32), p...  94.6 us
    pallas_call x1, Pallas kernels, local(): pl.pallas_call(final_kernel, out_shape=(jax.ShapeDtypeStruct((2, 256, 128...  2.32 us

profile of v4, /device:TPU:1, one launch (start us, length us, event | category | flops | bytes accessed | tf_op | source)
XLA Modules:
  0.0 97.5 jit_solution(10796642908910580102)
XLA Ops:
  0.6 94.6 %exchange.1 = (f32[2,256,1024]{2,1,0:T(8,128)S(1)}, f32[2,32,32,128]{3,2,1,0:T(8,128)S(1)}, f32[2,256,128]{2,1,0:T(8,128)S(1)}, f32[2,256,128]{2,1,0:T(8,128)S(1)}, f32[2,128,128]{2,1,0:T(8,128)S(1)}) custom-call(s32[2]{0:T(128)} %ranks.1, bf16[512,256]{1,0:T(8,128)(2,1)} %x_hbm.1, bf16[2,32,512]{2,1,0:T(8,128)(2,1)} %bitcast.1, f32[2,1,256,1024]{3,2,1,0:T(8,128)} %fb_hbm.1, ...), custom_call_target="tpu_custom_call" | custom-call | tf_op jit(solution)/shard_map/exchange/pallas_call | solution.py:444
  95.2 2.3 %finish.1 = (f32[2,256,128]{2,1,0:T(8,128)}, f32[2,1024,128]{2,1,0:T(8,128)}, f32[2,1,256,1024]{3,2,1,0:T(8,128)}) custom-call(f32[2,256,1024]{2,1,0:T(8,128)S(1)} %get-tuple-element.8.g, f32[2,32,32,128]{3,2,1,0:T(8,128)S(1)} %get-tuple-element.9.s, f32[2,256,128]{2,1,0:T(8,128)S(1)} %get-tuple-element.10.p, f32[2,256,128]{2,1,0:T(8,128)S(1)} %get-tuple-element.11.r, ...), custom_call_target="tpu_custom_call" | custom-call | tf_op jit(solution)/shard_map/finish/pallas_call | solution.py:490

commit v5 on v4

--- a/solution.py
+++ b/solution.py
@@ -50,7 +50,7 @@
 def comm_kernel(
     ranks, x_hbm, cot_hbm, fb_hbm, q_hbm,
     g_out, s_out, p_out, r_out, li_out,
-    xb, ct, fb, qv, gx, cf_h, cf_l, pp, pq, pr, rs, pf3, pf_x, s_src, s_rs, s_t, s_z, gl, g_rs, gg, mat,
+    xb, xt, ct, fb, qv, gx, cf_h, cf_l, pp, pq, pr, rs, pf3, pf_x, s_src, s_rs, s_t, s_z, gl, g_rs, gg, mat,
     l_sem, pr_send, pr_recv, a_send, a_recv, b_send, b_recv, z_send, z_recv, f_send, f_recv, near,
 ):
     z, c, x, y = (lax.axis_index(n) for n in ("z", "c", "x", "y"))
@@ -193,13 +193,17 @@
                 if s < last:
                     a_y(dirn, s + 1)
         for j in (s, NY - s) if s < 4 else (4,):
+            if s > 2:
+                k = chunk(0, 0, -j)
+                send(k, k, a_send.at[8 + j * 3 + 2], a_recv.at[8 + j * 3 + 2], at(dx=2))
             a_x(j, 1)
             a_x(j, -1)
 
     def a_far(j):
         d = far_dir(j)
         a_x_wait(j, d)
-        a_x_far(j)
+        if j not in (3, 4, 5):
+            a_x_far(j)
         a_x_wait(j, -d)
 
     def b_hop(s, dxs):
@@ -210,6 +214,8 @@
                     if s < b_reach(dx, dirn):
                         b_y(dx, dirn, s + 1)
 
+    loads[2].wait()
+    xt[...] = xb[...].astype(jnp.float32).T.astype(jnp.bfloat16)
     a_hop(1)
     for dx in (1, 3, 2):
         b_x_wait(dx)
@@ -225,9 +231,8 @@
         for j in {1: (0,), 2: (1, 7), 3: (2, 6), 4: (3, 5, 4)}[s]:
             a_far(j)
     told(5)
-    for cp in loads[2:]:
+    for cp in loads[3:]:
         cp.wait()
-    x_t = xb[...].astype(jnp.float32).T.astype(jnp.bfloat16)
     for j in (0, 1, 7, 2, 6, 3, 5, 4):
         a_x_far_wait(j)
 
@@ -238,7 +243,7 @@
         total = jnp.zeros((256, 128), jnp.float32)
         for b in range(NX):
             cols = pl.ds(b * 256, 256)
-            full = fb[m, 0, :, cols] + nt(x_t, ct[m, b].reshape(256, 512), None)
+            full = fb[m, 0, :, cols] + nt(xt[...], ct[m, b].reshape(256, 512), None)
             g_out[m, :, cols] = full
             total = total + three(nn, split(full), split(jnp.where(live, qv[m, cols, :], 0.0)))
         for i in range(NZ):
@@ -285,13 +290,13 @@
     left = pf3[...].reshape(NZ * PIECE, 128)[:256]
 
     f_sems = (f_send, f_recv)
+    left_parts = split(left)
     gram = nn(left.T, left)
     for i in range(NF):
         gl[i] = gram[4 * i : 4 * i + 4]
     for n, (dx, dy) in enumerate(OFFS):
         to = lax.rem(x + dx, NX) * NY + lax.rem(y + dy, NY)
         batch(gl.at[to], g_rs.at[n], f_sems, 0, at(dx=dx, dy=dy))
-    left_parts = split(left)
     for b in range(NX):
         rows = pl.ds(b * 256, 256)
         s_src[pl.ds(b * NY, NY)] = three(nn, (cf_h[rows, :], cf_l[rows, :]), left_parts).reshape(NY, 32, 128)
@@ -454,6 +459,7 @@
         out_specs=(vm,) * 5,
         scratch_shapes=[
             pltpu.VMEM((512, 256), b16),
+            pltpu.VMEM((256, 512), b16),
             pltpu.VMEM((2, NX, NY, 32, 512), b16),
             pltpu.VMEM((2, 1, 256, 1024), f32),
             pltpu.VMEM((2, 1024, 128), f32),

time: 97.7 us -> 93.9 us (0.961)
  Pallas kernels: 96.9 us -> 93.1 us
    pallas_call x1, Pallas kernels: 94.6 us -> 90.8 us  [local(): pl.pallas_call(comm_kernel, out_shape=(pltpu.VMEM((2, 256, 1024), f32), p...]
where the time goes in v5:
time: 93.9 us; the launch traced here: 93.7 us
  Pallas kernels  93.1 us (99%)
    pallas_call x1, Pallas kernels, local(): pl.pallas_call(comm_kernel, out_shape=(pltpu.VMEM((2, 256, 1024), f32), p...  90.8 us
    pallas_call x1, Pallas kernels, local(): pl.pallas_call(final_kernel, out_shape=(jax.ShapeDtypeStruct((2, 256, 128...  2.32 us

profile of v5, /device:TPU:1, one launch (start us, length us, event | category | flops | bytes accessed | tf_op | source)
XLA Modules:
  0.0 93.7 jit_solution(16749008224977591650)
XLA Ops:
  0.6 90.8 %exchange.1 = (f32[2,256,1024]{2,1,0:T(8,128)S(1)}, f32[2,32,32,128]{3,2,1,0:T(8,128)S(1)}, f32[2,256,128]{2,1,0:T(8,128)S(1)}, f32[2,256,128]{2,1,0:T(8,128)S(1)}, f32[2,128,128]{2,1,0:T(8,128)S(1)}) custom-call(s32[2]{0:T(128)} %ranks.1, bf16[512,256]{1,0:T(8,128)(2,1)} %x_hbm.1, bf16[2,32,512]{2,1,0:T(8,128)(2,1)} %bitcast.1, f32[2,1,256,1024]{3,2,1,0:T(8,128)} %fb_hbm.1, ...), custom_call_target="tpu_custom_call" | custom-call | tf_op jit(solution)/shard_map/exchange/pallas_call | solution.py:449
  91.4 2.3 %finish.1 = (f32[2,256,128]{2,1,0:T(8,128)}, f32[2,1024,128]{2,1,0:T(8,128)}, f32[2,1,256,1024]{3,2,1,0:T(8,128)}) custom-call(f32[2,256,1024]{2,1,0:T(8,128)S(1)} %get-tuple-element.8.g, f32[2,32,32,128]{3,2,1,0:T(8,128)S(1)} %get-tuple-element.9.s, f32[2,256,128]{2,1,0:T(8,128)S(1)} %get-tuple-element.10.p, f32[2,256,128]{2,1,0:T(8,128)S(1)} %get-tuple-element.11.r, ...), custom_call_target="tpu_custom_call" | custom-call | tf_op jit(solution)/shard_map/finish/pallas_call | solution.py:496
